TPU v7x, 256 devices: a whole 4x4x8 slice. The times are simulated.
256 devices in a mesh: row: 16 (over y_hi, x, core), col: 16 (over y_lo, z).
Axes of the slice: x: 4, y: 4 (y_hi: 2, y_lo: 2; y = y_hi * 2 + y_lo), z: 8, core: 2. Of those that a mesh axis runs over, the one named last changes fastest.
Arguments:
- tokens: bfloat16 [8192, 6144], P('row', 'col'), may hold values from -6 to 6
- gate_weight: bfloat16 [6144, 12288], P('row', 'col'), may hold values from -0.078125 to 0.078125
- up_weight: bfloat16 [6144, 12288], P('row', 'col'), may hold values from -0.078125 to 0.078125
Outputs:
- hidden: float32 [8192, 12288], P('row', 'col')
All inputs are finite; a program needn't handle non-finite values.
Results may differ from a plain program's by a relative error of at most 0.0003.
Values may be sent and summed in bfloat16 or wider, within the bound.
No kernel may reach another device: no remote copies, remote signals or barrier semaphores. Data moves between devices by JAX's collectives and lax.ppermute only.
A program may use at most 128 MiB of HBM per device.

v0:
```python
import jax
import jax.numpy as jnp
from jax import lax
from jax.sharding import PartitionSpec as P


def accumulate(gathered, weight_rows):
    return jnp.dot(gathered, weight_rows, preferred_element_type=jnp.float32)


def per_device(tokens, gate_weight, up_weight):
    gathered = lax.all_gather(tokens, "col", axis=1, tiled=True)

    def add_single(weight_rows):
        return accumulate(gathered, weight_rows)

    gate_sum = add_single(lax.all_gather(gate_weight, "row", axis=0, tiled=True))
    up_sum = add_single(lax.all_gather(up_weight, "row", axis=0, tiled=True))
    return jax.nn.silu(gate_sum) * up_sum


def solution(mesh):
    in_specs = (P("row", "col"), P("row", "col"), P("row", "col"))
    out_specs = P("row", "col")
    return jax.shard_map(
        per_device, mesh=mesh, in_specs=in_specs, out_specs=out_specs, check_vma=False
    )
```

profile of v0, /device:TPU:1, one launch (start us, length us, event | category | flops | bytes accessed | tf_op | source)
XLA Modules:
  0.0 278.8 jit_solution(5414926896950332376)
XLA Ops:
  6.5 0.0 all-gather.4.cloned.1.call-start
  6.5 0.7 all-gather.4.cloned.1.call-update
  7.3 0.0 all-gather.6.cloned.1.call-start
  7.3 0.7 all-gather.6.cloned.1.call-update
  8.0 0.0 all-gather.8.cloned.1.call-start
  8.1 0.7 all-gather.8.cloned.1.call-update
  8.7 82.3 %all-gather.4.cloned.1.call-done = bf16[512,6144]{1,0:T(8,128)(2,1)} async-done(((bf16[512,384]{1,0:T(8,128)(2,1)}), bf16[512,6144]{1,0:T(8,128)(2,1)}) %all-gather.4.cloned.1.call-update) | async-done | bytes 6291472 | tf_op jit(solution)/shard_map/all_gather | solution.py:12
  91.1 87.6 %all-gather.6.cloned.1.call-done = bf16[6144,768]{1,0:T(8,128)(2,1)} async-done(((bf16[384,768]{1,0:T(8,128)(2,1)}), bf16[6144,768]{1,0:T(8,128)(2,1)}) %all-gather.6.cloned.1.call-update) | async-done | bytes 9437200 | tf_op jit(solution)/shard_map/all_gather | solution.py:17
  178.6 9.3 %fusion = f32[512,768]{1,0:T(8,128)S(1)} fusion(bf16[512,6144]{1,0:T(8,128)(2,1)} %all-gather.4.cloned.1.call-done, bf16[6144,768]{1,0:T(8,128)(2,1)} %all-gather.6.cloned.1.call-done), kind=kOutput, calls=%fused_computation.1 | convolution fusion | flops 4831838208 | bytes 17301504 | tf_op jit(solution)/shard_map/dot_general | solution.py:8
  188.0 73.5 %all-gather.8.cloned.1.call-done = bf16[6144,768]{1,0:T(8,128)(2,1)} async-done(((bf16[384,768]{1,0:T(8,128)(2,1)}), bf16[6144,768]{1,0:T(8,128)(2,1)}) %all-gather.8.cloned.1.call-update) | async-done | bytes 9437200 | tf_op jit(solution)/shard_map/all_gather | solution.py:18
  261.5 10.7 %multiply_multiply_fusion = f32[512,768]{1,0:T(8,128)} fusion(f32[512,768]{1,0:T(8,128)S(1)} %fusion, bf16[512,6144]{1,0:T(8,128)(2,1)} %all-gather.4.cloned.1.call-done, bf16[6144,768]{1,0:T(8,128)(2,1)} %all-gather.8.cloned.1.call-done), kind=kOutput, calls=%fused_computation | convolution fusion | flops 4833804288 | bytes 18874368 | tf_op jit(solution)/shard_map/dot_general | solution.py:8
Async XLA Ops:
  6.5 84.5 %all-gather.4.cloned.1.call-start = ((), (), s32[]{:S(2)}) async-start(), calls=%async_computation | async-start | bytes 6684672 | tf_op jit(solution)/shard_map/all_gather | solution.py:12
  7.3 171.4 %all-gather.6.cloned.1.call-start = ((), (), s32[]{:S(2)}) async-start(), calls=%async_computation.1 | async-start | bytes 10027008 | tf_op jit(solution)/shard_map/all_gather | solution.py:17
  8.0 253.5 %all-gather.8.cloned.1.call-start = ((), (), s32[]{:S(2)}) async-start(), calls=%async_computation.2 | async-start | bytes 10027008 | tf_op jit(solution)/shard_map/all_gather | solution.py:18
Sparse Core Ops, SparseCore 0:
  9.2 81.8 all-gather.3
  93.8 84.7 all-gather.5
  181.4 80.0 all-gather.7
where the time goes:
time: 279 us
  waiting for transfers between devices  246 us (88%)
  matrix products  20.1 us (7%)
  between operations  13.1 us (5%)
    all_gather x1, waiting for transfers between devices, per_device(): lax.all_gather(gate_weight, 'row', axis=0, tiled=True)  87.6 us
    all_gather x1, waiting for transfers between devices, per_device(): gathered = lax.all_gather(tokens, 'col', axis=1, tiled=True)  82.3 us
    all_gather x1, waiting for transfers between devices, per_device(): up_sum = add_single(lax.all_gather(up_weight, 'row', axis=0, tiled=True))  73.5 us
    dot_general x2, matrix products, accumulate(): return jnp.dot(gathered, weight_rows, preferred_element_type=jnp.float32)  20.1 us
  transfers between devices with their start and end apart: 3, of which 3 were waited for; matrix products, arithmetic and copies ran while one was open for 3% of the time, Pallas kernels for 0%

commit v1 on v0

v1 whole, which is shorter than its diff:
```python
import functools

import jax
import jax.numpy as jnp
from jax import lax
from jax.experimental import pallas as pl
from jax.experimental.pallas import tpu as pltpu
from jax.sharding import Mesh
from jax.sharding import PartitionSpec as P

ROW = ("y_hi", "x", "core")
COL = ("y_lo", "z")


def shift(value, axis, size, by):
    return lax.ppermute(value, axis, [(i, (i + by) % size) for i in range(size)])


def multiply(origins, tokens_ref, *refs):
    y_hi, x, core = (lax.axis_index(name) for name in ROW)
    y_lo = lax.axis_index("y_lo")
    weights, hidden, tokens, held, gate, up, token_sem, weight_sem = refs[:16], *refs[16:]
    parts = len(weights) // 2
    depth = tokens_ref.shape[2]

    def token_copy(r, half):
        flip, offset = origins[r]
        from_core = core if half == 0 else 1 - core
        from_z = 2 * lax.rem(x + offset, 4) + from_core
        from_y = lax.rem(y_hi + flip + y_lo, 2)
        return pltpu.make_async_copy(
            tokens_ref.at[2 * from_z + from_y],
            tokens.at[r, :, pl.ds(half * depth, depth)],
            token_sem.at[r, half],
        )

    def weight_copy(r, half):
        return pltpu.make_async_copy(
            weights[2 * r + half],
            held.at[r, :, pl.ds(half * depth, depth), :],
            weight_sem.at[r, half],
        )

    for r in range(parts):
        for half in range(2):
            token_copy(r, half).start()
            weight_copy(r, half).start()
    for r in range(parts):
        for half in range(2):
            token_copy(r, half).wait()
            weight_copy(r, half).wait()
        gate_part = jnp.dot(tokens[r], held[r, 0], preferred_element_type=jnp.float32)
        up_part = jnp.dot(tokens[r], held[r, 1], preferred_element_type=jnp.float32)
        if r == 0:
            gate[...] = gate_part
            up[...] = up_part
        else:
            gate[...] += gate_part
            up[...] += up_part
    value = gate[...]
    hidden[...] = value / (1.0 + jnp.exp(-value)) * up[...]


def per_device(tokens, gate_weight, up_weight):
    rows, depth = tokens.shape
    width = gate_weight.shape[1]

    own = jnp.stack([gate_weight, up_weight])
    own, tokens = lax.optimization_barrier((own, tokens))
    other_tokens = shift(tokens, "y_lo", 2, 1)
    across = shift(own, "y_hi", 2, 1)
    own_2 = shift(own, "x", 4, 2)
    own_1 = shift(own, "x", 4, 1)
    own_3 = shift(own, "x", 4, -1)
    pair = jnp.stack([tokens, other_tokens])
    gathered = lax.all_gather(pair, "z", axis=0, tiled=True)
    across_1 = shift(across, "x", 4, 1)
    across_3 = shift(across, "x", 4, -1)
    across_2 = shift(own_2, "y_hi", 2, 1)

    blocks = [
        (0, 0, own),
        (0, 3, own_1),
        (0, 1, own_3),
        (0, 2, own_2),
        (1, 0, across),
        (1, 3, across_1),
        (1, 1, across_3),
        (1, 2, across_2),
    ]
    weights = []
    for _, _, block in blocks:
        weights += [block, shift(block, "core", 2, 1)]
    origins = tuple((flip, offset) for flip, offset, _ in blocks)
    parts = len(blocks)
    anywhere = pl.BlockSpec(memory_space=pl.ANY)
    return pl.pallas_call(
        functools.partial(multiply, origins),
        out_shape=jax.ShapeDtypeStruct((rows, width), jnp.float32),
        in_specs=[anywhere] * (1 + 2 * parts),
        out_specs=pl.BlockSpec(memory_space=pltpu.VMEM),
        scratch_shapes=[
            pltpu.VMEM((parts, rows, 2 * depth), tokens.dtype),
            pltpu.VMEM((parts, 2, 2 * depth, width), gate_weight.dtype),
            pltpu.VMEM((rows, width), jnp.float32),
            pltpu.VMEM((rows, width), jnp.float32),
            pltpu.SemaphoreType.DMA((parts, 2)),
            pltpu.SemaphoreType.DMA((parts, 2)),
        ],
        compiler_params=pltpu.CompilerParams(vmem_limit_bytes=48 * 1024 * 1024),
        cost_estimate=pl.CostEstimate(
            flops=4 * rows * width * depth * 16,
            bytes_accessed=2 * depth * 16 * (rows + 2 * width) + 4 * rows * width,
            transcendentals=rows * width,
        ),
    )(gathered, *weights)


def solution(mesh):
    fine = Mesh(mesh.devices.reshape(2, 4, 2, 2, 8), ROW + COL)
    spec = P(ROW, COL)
    return jax.shard_map(
        per_device, mesh=fine, in_specs=(spec,) * 3, out_specs=spec, check_vma=False
    )
```

time: 279 us -> 138 us (0.49)
  waiting for transfers between devices: 246 us -> 78.1 us
  starting transfers between devices: 0.08 us -> 24.3 us
  matrix products: 20.1 us -> 0 us
  Pallas kernels: 0 us -> 13.5 us
  local copies, waits for them, and re-layouts: 0 us -> 5.83 us
    all_gather x3 -> x1, waiting for transfers between devices: 243 us -> 0.01 us  [per_device(): gathered = lax.all_gather(pair, 'z', axis=0, tiled=True)]
    ppermute x0 -> x16, waiting for transfers between devices: none -> 78 us  [shift(): lax.ppermute(value, axis, [(i, (i + by) % size) for i in range(size)])]
    ppermute x0 -> x16, starting transfers between devices: none -> 24.3 us  [shift(): lax.ppermute(value, axis, [(i, (i + by) % size) for i in range(size)])]
    dot_general x2 -> x0, matrix products: 20.1 us -> none  [accumulate(): return jnp.dot(gathered, weight_rows, preferred_element_type=jnp.float32)]
    pallas_call x0 -> x1, Pallas kernels: none -> 13.5 us  [per_device(): pl.pallas_call(functools.partial(multiply, origins), out_shape=jax.ShapeD...]
    unnamed x0 -> x30, local copies, waits for them, and re-layouts: none -> 5.83 us
  transfers between devices with their start and end apart: 3 -> 17, of which waited for: 3 -> 8; matrix products, arithmetic and copies ran while one was open for 3% -> 0% of each run, Pallas kernels for 0% -> 0%
where the time goes in v1:
time: 138 us
  waiting for transfers between devices  78.1 us (57%)
  starting transfers between devices  24.3 us (18%)
  Pallas kernels  13.5 us (10%)
  between operations  13.5 us (10%)
  local copies, waits for them, and re-layouts  5.83 us (4%)
  other arithmetic  2.38 us (2%)
    ppermute x16, waiting for transfers between devices, shift(): lax.ppermute(value, axis, [(i, (i + by) % size) for i in range(size)])  78 us
    ppermute x16, starting transfers between devices, shift(): lax.ppermute(value, axis, [(i, (i + by) % size) for i in range(size)])  24.3 us
    pallas_call x1, Pallas kernels, per_device(): pl.pallas_call(functools.partial(multiply, origins), out_shape=jax.ShapeD...  13.5 us
    unnamed x30, local copies, waits for them, and re-layouts  5.83 us
  transfers between devices with their start and end apart: 17, of which 8 were waited for; matrix products, arithmetic and copies ran while one was open for 0% of the time, Pallas kernels for 0%

profile of v1, /device:TPU:1, one launch (start us, length us, event | category | flops | bytes accessed | tf_op | source)
XLA Modules:
  0.0 137.6 jit_solution(7753968396566014517)
XLA Ops:
  6.5 0.0 all-gather.2.cloned.1.call-start
  6.5 0.0 copy-start.4
  6.5 1.4 %pad_maximum_fusion.refs_0_ = bf16[2,384,768]{2,1,0:T(8,128)(2,1)S(1)} fusion(bf16[1,384,768]{2,1,0:T(8,128)(2,1)} %bitcast.4, bf16[1,384,768]{2,1,0:T(8,128)(2,1)} %bitcast.5), kind=kLoop, calls=%fused_computation | loop fusion | flops 589824 | bytes 2359296 | tf_op jit(solution)/shard_map/stack | solution.py:68
  7.9 0.0 copy-done.4
  8.0 2.2 %collective-permute-start = (bf16[512,384]{1,0:T(8,128)(2,1)S(1)}, bf16[512,384]{1,0:T(8,128)(2,1)S(1)}, u32[]{:S(2)}, u32[]{:S(2)}) collective-permute-start(bf16[512,384]{1,0:T(8,128)(2,1)S(1)} %copy-done.4), channel_id=1, source_target_pairs={{0,8},{8,0},{1,9},{9,1},{2,10},{10,2},{3,11},{11,3},{4,12},{12,4},... | collective-permute-start | bytes 1179656 | tf_op jit(solution)/shard_map/ppermute | solution.py:16
  10.2 7.6 %collective-permute-done = bf16[512,384]{1,0:T(8,128)(2,1)S(1)} collective-permute-done((bf16[512,384]{1,0:T(8,128)(2,1)S(1)}, bf16[512,384]{1,0:T(8,128)(2,1)S(1)}, u32[]{:S(2)}, u32[]{:S(2)}) %collective-permute-start) | collective-permute-done | bytes 393248 | tf_op jit(solution)/shard_map/ppermute | solution.py:16
  17.8 1.0 pad_maximum_fusion.1
  18.7 0.0 all-gather.2.cloned.1.call-update
  18.8 4.1 %collective-permute-start.8 = (bf16[2,384,768]{2,1,0:T(8,128)(2,1)S(1)}, bf16[2,384,768]{2,1,0:T(8,128)(2,1)S(1)}, u32[]{:S(2)}, u32[]{:S(2)}) collective-permute-start(bf16[2,384,768]{2,1,0:T(8,128)(2,1)S(1)} %pad_maximum_fusion.refs_0_), channel_id=1, source_target_pairs={{0,128},{128,0},{1,129},{129,1},{2,130},{130,2},{3,131},{131,3},{4... | collective-permute-start | bytes 3538952 | tf_op jit(solution)/shard_map/ppermute | solution.py:16
  22.9 2.7 %collective-permute-start.6 = (bf16[2,384,768]{2,1,0:T(8,128)(2,1)S(1)}, bf16[2,384,768]{2,1,0:T(8,128)(2,1)S(1)}, u32[]{:S(2)}, u32[]{:S(2)}) collective-permute-start(bf16[2,384,768]{2,1,0:T(8,128)(2,1)S(1)} %pad_maximum_fusion.refs_0_), channel_id=1, source_target_pairs={{0,64},{32,96},{64,0},{96,32},{1,65},{33,97},{65,1},{97,33},{2,66}... | collective-permute-start | bytes 3538952 | tf_op jit(solution)/shard_map/ppermute | solution.py:16
  25.6 0.9 collective-permute-start.4
  26.5 0.6 collective-permute-start.2
  27.1 2.7 %collective-permute-start.1 = (bf16[2,384,768]{2,1,0:T(8,128)(2,1)S(1)}, bf16[2,384,768]{2,1,0:T(8,128)(2,1)S(1)}, u32[]{:S(2)}, u32[]{:S(2)}) collective-permute-start(bf16[2,384,768]{2,1,0:T(8,128)(2,1)S(1)} %pad_maximum_fusion.refs_0_), channel_id=1, source_target_pairs={{0,16},{16,0},{1,17},{17,1},{2,18},{18,2},{3,19},{19,3},{4,20},{20... | collective-permute-start | bytes 3538952 | tf_op jit(solution)/shard_map/ppermute | solution.py:16
  29.7 17.7 %collective-permute-done.8.refs_8_ = bf16[2,384,768]{2,1,0:T(8,128)(2,1)S(1)} collective-permute-done((bf16[2,384,768]{2,1,0:T(8,128)(2,1)S(1)}, bf16[2,384,768]{2,1,0:T(8,128)(2,1)S(1)}, u32[]{:S(2)}, u32[]{:S(2)}) %collective-permute-start.8) | collective-permute-done | bytes 1179680 | tf_op jit(solution)/shard_map/ppermute | solution.py:16
  47.4 2.4 %collective-permute-start.12 = (bf16[2,384,768]{2,1,0:T(8,128)(2,1)S(1)}, bf16[2,384,768]{2,1,0:T(8,128)(2,1)S(1)}, u32[]{:S(2)}, u32[]{:S(2)}) collective-permute-start(bf16[2,384,768]{2,1,0:T(8,128)(2,1)S(1)} %collective-permute-done.8.refs_8_), channel_id=1, source_target_pairs={{0,96},{32,0},{64,32},{96,64},{1,97},{33,1},{65,33},{97,65},{2,98}... | collective-permute-start | bytes 3538952 | tf_op jit(solution)/shard_map/ppermute | solution.py:16
  49.8 0.2 collective-permute-done.6.refs_6_
  50.0 0.0 copy-start.6
  50.0 1.4 collective-permute-start.10
  51.4 25.2 %collective-permute-done.4.refs_4_ = bf16[2,384,768]{2,1,0:T(8,128)(2,1)S(1)} collective-permute-done((bf16[2,384,768]{2,1,0:T(8,128)(2,1)S(1)}, bf16[2,384,768]{2,1,0:T(8,128)(2,1)S(1)}, u32[]{:S(2)}, u32[]{:S(2)}) %collective-permute-start.4) | collective-permute-done | bytes 1179680 | tf_op jit(solution)/shard_map/ppermute | solution.py:16
  76.6 3.9 %collective-permute-start.9 = (bf16[2,384,768]{2,1,0:T(8,128)(2,1)S(1)}, bf16[2,384,768]{2,1,0:T(8,128)(2,1)S(1)}, u32[]{:S(2)}, u32[]{:S(2)}) collective-permute-start(bf16[2,384,768]{2,1,0:T(8,128)(2,1)S(1)} %collective-permute-done.8.refs_8_), channel_id=1, source_target_pairs={{0,16},{16,0},{1,17},{17,1},{2,18},{18,2},{3,19},{19,3},{4,20},{20... | collective-permute-start | bytes 3538952 | tf_op jit(solution)/shard_map/ppermute | solution.py:16
  80.5 0.0 collective-permute-done.2.refs_2_
  80.5 0.1 collective-permute-start.14
  80.6 0.0 collective-permute-done.1.refs_1_
  80.6 0.0 copy-start
  80.6 1.0 copy-done
  81.6 0.3 collective-permute-start.7
  81.9 20.0 %collective-permute-done.12.refs_12_ = bf16[2,384,768]{2,1,0:T(8,128)(2,1)S(1)} collective-permute-done((bf16[2,384,768]{2,1,0:T(8,128)(2,1)S(1)}, bf16[2,384,768]{2,1,0:T(8,128)(2,1)S(1)}, u32[]{:S(2)}, u32[]{:S(2)}) %collective-permute-start.12) | collective-permute-done | bytes 1179680 | tf_op jit(solution)/shard_map/ppermute | solution.py:16
  101.9 0.0 copy-start.7
  101.9 1.6 %collective-permute-start.5 = (bf16[2,384,768]{2,1,0:T(8,128)(2,1)S(1)}, bf16[2,384,768]{2,1,0:T(8,128)(2,1)S(1)}, u32[]{:S(2)}, u32[]{:S(2)}) collective-permute-start(bf16[2,384,768]{2,1,0:T(8,128)(2,1)S(1)} %collective-permute-done.4.refs_4_), channel_id=1, source_target_pairs={{0,16},{16,0},{1,17},{17,1},{2,18},{18,2},{3,19},{19,3},{4,20},{20... | collective-permute-start | bytes 3538952 | tf_op jit(solution)/shard_map/ppermute | solution.py:16
  103.4 0.0 collective-permute-done.10.refs_10_
  103.4 0.0 copy-start.8
  103.4 0.1 collective-permute-start.3
  103.5 0.0 collective-permute-done.9.refs_9_
  103.5 0.0 copy-start.9
  103.5 0.4 collective-permute-start.13
  104.0 5.7 %collective-permute-done.14.refs_14_ = bf16[2,384,768]{2,1,0:T(8,128)(2,1)S(1)} collective-permute-done((bf16[2,384,768]{2,1,0:T(8,128)(2,1)S(1)}, bf16[2,384,768]{2,1,0:T(8,128)(2,1)S(1)}, u32[]{:S(2)}, u32[]{:S(2)}) %collective-permute-start.14) | collective-permute-done | bytes 1179680 | tf_op jit(solution)/shard_map/ppermute | solution.py:16
  109.6 0.0 copy-start.10
  109.6 0.8 collective-permute-start.11
  110.4 0.0 collective-permute-done.7.refs_7_
  110.4 0.0 copy-start.11
  110.4 0.3 collective-permute-start.15
  110.7 0.0 collective-permute-done.5.refs_5_
  110.7 0.0 copy-start.12
  110.7 0.0 collective-permute-done.3.refs_3_
  110.7 0.0 copy-done.5
  110.7 0.0 copy-start.2
  110.7 1.2 copy-done.2
  111.9 0.0 collective-permute-done.13.refs_13_
  111.9 0.0 copy-done.6
  111.9 0.0 copy-start.13
  111.9 1.0 collective-permute-done.11.refs_11_
  112.9 0.0 copy-done.7
  112.9 0.0 copy-done.8
  112.9 0.0 copy-done.9
  112.9 0.0 copy-done.10
  112.9 0.0 copy-done.11
  112.9 0.0 copy-done.12
  112.9 0.0 copy-done.13
  112.9 0.0 copy-start.14
  112.9 1.0 copy-done.14
  114.0 0.7 collective-permute-done.15.refs_15_
  114.7 1.3 copy-done.1
  116.0 1.3 copy-done.3
  117.2 13.5 %shard_map.37 = f32[512,768]{1,0:T(8,128)} custom-call(bf16[16,512,384]{2,1,0:T(8,128)(2,1)} %all-gather.2.cloned.1.call-done.tokens_ref, bf16[2,384,768]{2,1,0:T(8,128)(2,1)S(1)} %pad_maximum_fusion.refs_0_, bf16[2,384,768]{2,1,0:T(8,128)(2,1)S(1)} %copy-done.1, bf16[2,384,768]{2,1,0:T(8,128)(2,1)S(1)} %collective-permute-done.2.refs_2_, ...), custom_call_target="tpu_custom_call" | custom-call | flops 9663676416 | bytes 26738688 | tf_op jit(solution)/shard_map/pallas_call | solution.py:97
  (4 shorter events, 0.0 us)
Async XLA Ops:
  6.5 108.2 %all-gather.2.cloned.1.call-start = ((), (), s32[]{:S(2)}) async-start(), calls=%async_computation | async-start | bytes 7077888 | tf_op jit(solution)/shard_map/all_gather | solution.py:76
  6.5 1.4 %copy-start.4 = (bf16[512,384]{1,0:T(8,128)(2,1)S(1)}, bf16[512,384]{1,0:T(8,128)(2,1)}, u32[]{:S(2)}) copy-start(bf16[512,384]{1,0:T(8,128)(2,1)} %param.3) | copy-start | bytes 1179652
  8.0 9.8 %collective-permute-start = (bf16[512,384]{1,0:T(8,128)(2,1)S(1)}, bf16[512,384]{1,0:T(8,128)(2,1)S(1)}, u32[]{:S(2)}, u32[]{:S(2)}) collective-permute-start(bf16[512,384]{1,0:T(8,128)(2,1)S(1)} %copy-done.4), channel_id=1, source_target_pairs={{0,8},{8,0},{1,9},{9,1},{2,10},{10,2},{3,11},{11,3},{4,12},{12,4},... | collective-permute-start | bytes 1179656 | tf_op jit(solution)/shard_map/ppermute | solution.py:16
  18.8 28.7 %collective-permute-start.8 = (bf16[2,384,768]{2,1,0:T(8,128)(2,1)S(1)}, bf16[2,384,768]{2,1,0:T(8,128)(2,1)S(1)}, u32[]{:S(2)}, u32[]{:S(2)}) collective-permute-start(bf16[2,384,768]{2,1,0:T(8,128)(2,1)S(1)} %pad_maximum_fusion.refs_0_), channel_id=1, source_target_pairs={{0,128},{128,0},{1,129},{129,1},{2,130},{130,2},{3,131},{131,3},{4... | collective-permute-start | bytes 3538952 | tf_op jit(solution)/shard_map/ppermute | solution.py:16
  22.9 27.2 %collective-permute-start.6 = (bf16[2,384,768]{2,1,0:T(8,128)(2,1)S(1)}, bf16[2,384,768]{2,1,0:T(8,128)(2,1)S(1)}, u32[]{:S(2)}, u32[]{:S(2)}) collective-permute-start(bf16[2,384,768]{2,1,0:T(8,128)(2,1)S(1)} %pad_maximum_fusion.refs_0_), channel_id=1, source_target_pairs={{0,64},{32,96},{64,0},{96,32},{1,65},{33,97},{65,1},{97,33},{2,66}... | collective-permute-start | bytes 3538952 | tf_op jit(solution)/shard_map/ppermute | solution.py:16
  25.6 51.0 %collective-permute-start.4 = (bf16[2,384,768]{2,1,0:T(8,128)(2,1)S(1)}, bf16[2,384,768]{2,1,0:T(8,128)(2,1)S(1)}, u32[]{:S(2)}, u32[]{:S(2)}) collective-permute-start(bf16[2,384,768]{2,1,0:T(8,128)(2,1)S(1)} %pad_maximum_fusion.refs_0_), channel_id=1, source_target_pairs={{0,96},{32,0},{64,32},{96,64},{1,97},{33,1},{65,33},{97,65},{2,98}... | collective-permute-start | bytes 3538952 | tf_op jit(solution)/shard_map/ppermute | solution.py:16
  26.5 54.0 %collective-permute-start.2 = (bf16[2,384,768]{2,1,0:T(8,128)(2,1)S(1)}, bf16[2,384,768]{2,1,0:T(8,128)(2,1)S(1)}, u32[]{:S(2)}, u32[]{:S(2)}) collective-permute-start(bf16[2,384,768]{2,1,0:T(8,128)(2,1)S(1)} %pad_maximum_fusion.refs_0_), channel_id=1, source_target_pairs={{0,32},{32,64},{64,96},{96,0},{1,33},{33,65},{65,97},{97,1},{2,34}... | collective-permute-start | bytes 3538952 | tf_op jit(solution)/shard_map/ppermute | solution.py:16
  27.1 53.5 %collective-permute-start.1 = (bf16[2,384,768]{2,1,0:T(8,128)(2,1)S(1)}, bf16[2,384,768]{2,1,0:T(8,128)(2,1)S(1)}, u32[]{:S(2)}, u32[]{:S(2)}) collective-permute-start(bf16[2,384,768]{2,1,0:T(8,128)(2,1)S(1)} %pad_maximum_fusion.refs_0_), channel_id=1, source_target_pairs={{0,16},{16,0},{1,17},{17,1},{2,18},{18,2},{3,19},{19,3},{4,20},{20... | collective-permute-start | bytes 3538952 | tf_op jit(solution)/shard_map/ppermute | solution.py:16
  47.4 63.3 %copy-start.5 = (bf16[2,384,768]{2,1,0:T(8,128)(2,1)}, bf16[2,384,768]{2,1,0:T(8,128)(2,1)S(1)}, u32[]{:S(2)}) copy-start(bf16[2,384,768]{2,1,0:T(8,128)(2,1)S(1)} %collective-permute-done.8.refs_8_) | copy-start | bytes 3538948
  47.4 54.5 %collective-permute-start.12 = (bf16[2,384,768]{2,1,0:T(8,128)(2,1)S(1)}, bf16[2,384,768]{2,1,0:T(8,128)(2,1)S(1)}, u32[]{:S(2)}, u32[]{:S(2)}) collective-permute-start(bf16[2,384,768]{2,1,0:T(8,128)(2,1)S(1)} %collective-permute-done.8.refs_8_), channel_id=1, source_target_pairs={{0,96},{32,0},{64,32},{96,64},{1,97},{33,1},{65,33},{97,65},{2,98}... | collective-permute-start | bytes 3538952 | tf_op jit(solution)/shard_map/ppermute | solution.py:16
  50.0 61.9 %copy-start.6 = (bf16[2,384,768]{2,1,0:T(8,128)(2,1)}, bf16[2,384,768]{2,1,0:T(8,128)(2,1)S(1)}, u32[]{:S(2)}) copy-start(bf16[2,384,768]{2,1,0:T(8,128)(2,1)S(1)} %collective-permute-done.6.refs_6_) | copy-start | bytes 3538948
  50.0 53.4 %collective-permute-start.10 = (bf16[2,384,768]{2,1,0:T(8,128)(2,1)S(1)}, bf16[2,384,768]{2,1,0:T(8,128)(2,1)S(1)}, u32[]{:S(2)}, u32[]{:S(2)}) collective-permute-start(bf16[2,384,768]{2,1,0:T(8,128)(2,1)S(1)} %collective-permute-done.8.refs_8_), channel_id=1, source_target_pairs={{0,32},{32,64},{64,96},{96,0},{1,33},{33,65},{65,97},{97,1},{2,34}... | collective-permute-start | bytes 3538952 | tf_op jit(solution)/shard_map/ppermute | solution.py:16
  76.6 26.9 %collective-permute-start.9 = (bf16[2,384,768]{2,1,0:T(8,128)(2,1)S(1)}, bf16[2,384,768]{2,1,0:T(8,128)(2,1)S(1)}, u32[]{:S(2)}, u32[]{:S(2)}) collective-permute-start(bf16[2,384,768]{2,1,0:T(8,128)(2,1)S(1)} %collective-permute-done.8.refs_8_), channel_id=1, source_target_pairs={{0,16},{16,0},{1,17},{17,1},{2,18},{18,2},{3,19},{19,3},{4,20},{20... | collective-permute-start | bytes 3538952 | tf_op jit(solution)/shard_map/ppermute | solution.py:16
  80.5 29.1 %collective-permute-start.14 = (bf16[2,384,768]{2,1,0:T(8,128)(2,1)S(1)}, bf16[2,384,768]{2,1,0:T(8,128)(2,1)S(1)}, u32[]{:S(2)}, u32[]{:S(2)}) collective-permute-start(bf16[2,384,768]{2,1,0:T(8,128)(2,1)S(1)} %collective-permute-done.6.refs_6_), channel_id=1, source_target_pairs={{0,128},{128,0},{1,129},{129,1},{2,130},{130,2},{3,131},{131,3},{4... | collective-permute-start | bytes 3538952 | tf_op jit(solution)/shard_map/ppermute | solution.py:16
  80.6 1.0 copy-start
  81.6 28.8 %collective-permute-start.7 = (bf16[2,384,768]{2,1,0:T(8,128)(2,1)S(1)}, bf16[2,384,768]{2,1,0:T(8,128)(2,1)S(1)}, u32[]{:S(2)}, u32[]{:S(2)}) collective-permute-start(bf16[2,384,768]{2,1,0:T(8,128)(2,1)S(1)} %collective-permute-done.6.refs_6_), channel_id=1, source_target_pairs={{0,16},{16,0},{1,17},{17,1},{2,18},{18,2},{3,19},{19,3},{4,20},{20... | collective-permute-start | bytes 3538952 | tf_op jit(solution)/shard_map/ppermute | solution.py:16
  101.9 11.0 %copy-start.7 = (bf16[2,384,768]{2,1,0:T(8,128)(2,1)}, bf16[2,384,768]{2,1,0:T(8,128)(2,1)S(1)}, u32[]{:S(2)}) copy-start(bf16[2,384,768]{2,1,0:T(8,128)(2,1)S(1)} %collective-permute-done.12.refs_12_) | copy-start | bytes 3538948
  101.9 8.8 %collective-permute-start.5 = (bf16[2,384,768]{2,1,0:T(8,128)(2,1)S(1)}, bf16[2,384,768]{2,1,0:T(8,128)(2,1)S(1)}, u32[]{:S(2)}, u32[]{:S(2)}) collective-permute-start(bf16[2,384,768]{2,1,0:T(8,128)(2,1)S(1)} %collective-permute-done.4.refs_4_), channel_id=1, source_target_pairs={{0,16},{16,0},{1,17},{17,1},{2,18},{18,2},{3,19},{19,3},{4,20},{20... | collective-permute-start | bytes 3538952 | tf_op jit(solution)/shard_map/ppermute | solution.py:16
  103.4 9.4 %copy-start.8 = (bf16[2,384,768]{2,1,0:T(8,128)(2,1)}, bf16[2,384,768]{2,1,0:T(8,128)(2,1)S(1)}, u32[]{:S(2)}) copy-start(bf16[2,384,768]{2,1,0:T(8,128)(2,1)S(1)} %collective-permute-done.10.refs_10_) | copy-start | bytes 3538948
  103.4 7.2 %collective-permute-start.3 = (bf16[2,384,768]{2,1,0:T(8,128)(2,1)S(1)}, bf16[2,384,768]{2,1,0:T(8,128)(2,1)S(1)}, u32[]{:S(2)}, u32[]{:S(2)}) collective-permute-start(bf16[2,384,768]{2,1,0:T(8,128)(2,1)S(1)} %collective-permute-done.2.refs_2_), channel_id=1, source_target_pairs={{0,16},{16,0},{1,17},{17,1},{2,18},{18,2},{3,19},{19,3},{4,20},{20... | collective-permute-start | bytes 3538952 | tf_op jit(solution)/shard_map/ppermute | solution.py:16
  103.5 9.3 %copy-start.9 = (bf16[2,384,768]{2,1,0:T(8,128)(2,1)}, bf16[2,384,768]{2,1,0:T(8,128)(2,1)S(1)}, u32[]{:S(2)}) copy-start(bf16[2,384,768]{2,1,0:T(8,128)(2,1)S(1)} %collective-permute-done.9.refs_9_) | copy-start | bytes 3538948
  103.5 8.4 %collective-permute-start.13 = (bf16[2,384,768]{2,1,0:T(8,128)(2,1)S(1)}, bf16[2,384,768]{2,1,0:T(8,128)(2,1)S(1)}, u32[]{:S(2)}, u32[]{:S(2)}) collective-permute-start(bf16[2,384,768]{2,1,0:T(8,128)(2,1)S(1)} %collective-permute-done.12.refs_12_), channel_id=1, source_target_pairs={{0,16},{16,0},{1,17},{17,1},{2,18},{18,2},{3,19},{19,3},{4,20},{20... | collective-permute-start | bytes 3538952 | tf_op jit(solution)/shard_map/ppermute | solution.py:16
  109.6 3.3 %copy-start.10 = (bf16[2,384,768]{2,1,0:T(8,128)(2,1)}, bf16[2,384,768]{2,1,0:T(8,128)(2,1)S(1)}, u32[]{:S(2)}) copy-start(bf16[2,384,768]{2,1,0:T(8,128)(2,1)S(1)} %collective-permute-done.14.refs_14_) | copy-start | bytes 3538948
  109.6 3.3 %collective-permute-start.11 = (bf16[2,384,768]{2,1,0:T(8,128)(2,1)S(1)}, bf16[2,384,768]{2,1,0:T(8,128)(2,1)S(1)}, u32[]{:S(2)}, u32[]{:S(2)}) collective-permute-start(bf16[2,384,768]{2,1,0:T(8,128)(2,1)S(1)} %collective-permute-done.10.refs_10_), channel_id=1, source_target_pairs={{0,16},{16,0},{1,17},{17,1},{2,18},{18,2},{3,19},{19,3},{4,20},{20... | collective-permute-start | bytes 3538952 | tf_op jit(solution)/shard_map/ppermute | solution.py:16
  110.4 2.5 %copy-start.11 = (bf16[2,384,768]{2,1,0:T(8,128)(2,1)}, bf16[2,384,768]{2,1,0:T(8,128)(2,1)S(1)}, u32[]{:S(2)}) copy-start(bf16[2,384,768]{2,1,0:T(8,128)(2,1)S(1)} %collective-permute-done.7.refs_7_) | copy-start | bytes 3538948
  110.4 4.3 %collective-permute-start.15 = (bf16[2,384,768]{2,1,0:T(8,128)(2,1)S(1)}, bf16[2,384,768]{2,1,0:T(8,128)(2,1)}, u32[]{:S(2)}, u32[]{:S(2)}) collective-permute-start(bf16[2,384,768]{2,1,0:T(8,128)(2,1)S(1)} %collective-permute-done.14.refs_14_), channel_id=1, source_target_pairs={{0,16},{16,0},{1,17},{17,1},{2,18},{18,2},{3,19},{19,3},{4,20},{20... | collective-permute-start | bytes 3538952 | tf_op jit(solution)/shard_map/ppermute | solution.py:16
  110.7 2.2 %copy-start.12 = (bf16[2,384,768]{2,1,0:T(8,128)(2,1)}, bf16[2,384,768]{2,1,0:T(8,128)(2,1)S(1)}, u32[]{:S(2)}) copy-start(bf16[2,384,768]{2,1,0:T(8,128)(2,1)S(1)} %collective-permute-done.5.refs_5_) | copy-start | bytes 3538948
  110.7 1.2 copy-start.2
  111.9 1.0 copy-start.13
  112.9 1.0 copy-start.14
  114.7 1.3 copy-start.1
  116.0 1.3 copy-start.3
Sparse Core Ops, SparseCore 0:
  18.9 79.4 all-gather.1

commit v2 on v1

--- a/solution.py
+++ b/solution.py
@@ -10,6 +10,7 @@
 
 ROW = ("y_hi", "x", "core")
 COL = ("y_lo", "z")
+AHEAD = 2
 
 
 def shift(value, axis, size, by):
@@ -41,14 +42,19 @@
             weight_sem.at[r, half],
         )
 
-    for r in range(parts):
+    def start(r):
         for half in range(2):
             token_copy(r, half).start()
             weight_copy(r, half).start()
+
+    for r in range(AHEAD):
+        start(r)
     for r in range(parts):
         for half in range(2):
             token_copy(r, half).wait()
             weight_copy(r, half).wait()
+        if r + AHEAD < parts:
+            start(r + AHEAD)
         gate_part = jnp.dot(tokens[r], held[r, 0], preferred_element_type=jnp.float32)
         up_part = jnp.dot(tokens[r], held[r, 1], preferred_element_type=jnp.float32)
         if r == 0:
@@ -69,9 +75,11 @@
     own, tokens = lax.optimization_barrier((own, tokens))
     other_tokens = shift(tokens, "y_lo", 2, 1)
     across = shift(own, "y_hi", 2, 1)
-    own_2 = shift(own, "x", 4, 2)
     own_1 = shift(own, "x", 4, 1)
     own_3 = shift(own, "x", 4, -1)
+    own_2g = shift(own_1[0], "x", 4, 1)
+    own_2u = shift(own_3[1], "x", 4, -1)
+    own_2 = jnp.stack([own_2g, own_2u])
     pair = jnp.stack([tokens, other_tokens])
     gathered = lax.all_gather(pair, "z", axis=0, tiled=True)
     across_1 = shift(across, "x", 4, 1)
@@ -107,7 +115,7 @@
             pltpu.SemaphoreType.DMA((parts, 2)),
             pltpu.SemaphoreType.DMA((parts, 2)),
         ],
-        compiler_params=pltpu.CompilerParams(vmem_limit_bytes=48 * 1024 * 1024),
+        compiler_params=pltpu.CompilerParams(vmem_limit_bytes=58 * 1024 * 1024),
         cost_estimate=pl.CostEstimate(
             flops=4 * rows * width * depth * 16,
             bytes_accessed=2 * depth * 16 * (rows + 2 * width) + 4 * rows * width,

time: 138 us -> 124 us (0.90)
  waiting for transfers between devices: 78.1 us -> 53.5 us
  starting transfers between devices: 24.3 us -> 38.2 us
  local copies, waits for them, and re-layouts: 5.83 us -> 2.09 us
    ppermute x16 -> x17, waiting for transfers between devices: 78 us -> 53.4 us  [shift(): lax.ppermute(value, axis, [(i, (i + by) % size) for i in range(size)])]
    ppermute x16 -> x17, starting transfers between devices: 24.3 us -> 38.2 us  [shift(): lax.ppermute(value, axis, [(i, (i + by) % size) for i in range(size)])]
    unnamed x30 -> x32, local copies, waits for them, and re-layouts: 5.83 us -> 2.01 us
  transfers between devices with their start and end apart: 17 -> 18, of which waited for: 8 -> 7; matrix products, arithmetic and copies ran while one was open for 0% -> 0% of each run, Pallas kernels for 0% -> 0%
where the time goes in v2:
time: 124 us
  waiting for transfers between devices  53.5 us (43%)
  starting transfers between devices  38.2 us (31%)
  Pallas kernels  14.2 us (11%)
  between operations  13.6 us (11%)
  other arithmetic  2.48 us (2%)
  local copies, waits for them, and re-layouts  2.09 us (2%)
    ppermute x17, waiting for transfers between devices, shift(): lax.ppermute(value, axis, [(i, (i + by) % size) for i in range(size)])  53.4 us
    ppermute x17, starting transfers between devices, shift(): lax.ppermute(value, axis, [(i, (i + by) % size) for i in range(size)])  38.2 us
    pallas_call x1, Pallas kernels, per_device(): pl.pallas_call(functools.partial(multiply, origins), out_shape=jax.ShapeD...  14.2 us
  transfers between devices with their start and end apart: 18, of which 7 were waited for; matrix products, arithmetic and copies ran while one was open for 0% of the time, Pallas kernels for 0%

profile of v2, /device:TPU:1, one launch (start us, length us, event | category | flops | bytes accessed | tf_op | source)
XLA Modules:
  0.0 124.1 jit_solution(12873892434453164523)
XLA Ops:
  6.5 0.0 all-gather.2.cloned.1.call-start
  6.5 0.0 copy-start.2
  6.5 1.4 %pad_maximum_fusion.refs_0_ = bf16[2,384,768]{2,1,0:T(8,128)(2,1)S(1)} fusion(bf16[1,384,768]{2,1,0:T(8,128)(2,1)} %bitcast.10, bf16[1,384,768]{2,1,0:T(8,128)(2,1)} %bitcast.11), kind=kLoop, calls=%fused_computation | loop fusion | flops 589824 | bytes 2359296 | tf_op jit(solution)/shard_map/stack | solution.py:74
  7.9 0.0 copy-done.2
  8.0 0.0 copy-start
  8.0 2.2 %collective-permute-start = (bf16[512,384]{1,0:T(8,128)(2,1)S(1)}, bf16[512,384]{1,0:T(8,128)(2,1)S(1)}, u32[]{:S(2)}, u32[]{:S(2)}) collective-permute-start(bf16[512,384]{1,0:T(8,128)(2,1)S(1)} %copy-done.2), channel_id=1, source_target_pairs={{0,8},{8,0},{1,9},{9,1},{2,10},{10,2},{3,11},{11,3},{4,12},{12,4},... | collective-permute-start | bytes 1179656 | tf_op jit(solution)/shard_map/ppermute | solution.py:17
  10.2 7.6 %collective-permute-done = bf16[512,384]{1,0:T(8,128)(2,1)S(1)} collective-permute-done((bf16[512,384]{1,0:T(8,128)(2,1)S(1)}, bf16[512,384]{1,0:T(8,128)(2,1)S(1)}, u32[]{:S(2)}, u32[]{:S(2)}) %collective-permute-start) | collective-permute-done | bytes 393248 | tf_op jit(solution)/shard_map/ppermute | solution.py:17
  17.8 1.0 pad_maximum_fusion.2
  18.7 0.0 all-gather.2.cloned.1.call-update
  18.8 3.7 %collective-permute-start.4 = (bf16[2,384,768]{2,1,0:T(8,128)(2,1)S(1)}, bf16[2,384,768]{2,1,0:T(8,128)(2,1)S(1)}, u32[]{:S(2)}, u32[]{:S(2)}) collective-permute-start(bf16[2,384,768]{2,1,0:T(8,128)(2,1)S(1)} %pad_maximum_fusion.refs_0_), channel_id=1, source_target_pairs={{0,96},{32,0},{64,32},{96,64},{1,97},{33,1},{65,33},{97,65},{2,98}... | collective-permute-start | bytes 3538952 | tf_op jit(solution)/shard_map/ppermute | solution.py:17
  22.4 0.0 collective-permute-start.2
  22.4 2.9 %collective-permute-start.9 = (bf16[2,384,768]{2,1,0:T(8,128)(2,1)S(1)}, bf16[2,384,768]{2,1,0:T(8,128)(2,1)S(1)}, u32[]{:S(2)}, u32[]{:S(2)}) collective-permute-start(bf16[2,384,768]{2,1,0:T(8,128)(2,1)S(1)} %pad_maximum_fusion.refs_0_), channel_id=1, source_target_pairs={{0,128},{128,0},{1,129},{129,1},{2,130},{130,2},{3,131},{131,3},{4... | collective-permute-start | bytes 3538952 | tf_op jit(solution)/shard_map/ppermute | solution.py:17
  25.3 0.0 copy-done
  25.3 2.1 %collective-permute-start.1 = (bf16[2,384,768]{2,1,0:T(8,128)(2,1)S(1)}, bf16[2,384,768]{2,1,0:T(8,128)(2,1)S(1)}, u32[]{:S(2)}, u32[]{:S(2)}) collective-permute-start(bf16[2,384,768]{2,1,0:T(8,128)(2,1)S(1)} %pad_maximum_fusion.refs_0_), channel_id=1, source_target_pairs={{0,16},{16,0},{1,17},{17,1},{2,18},{18,2},{3,19},{19,3},{4,20},{20... | collective-permute-start | bytes 3538952 | tf_op jit(solution)/shard_map/ppermute | solution.py:17
  27.4 18.7 %collective-permute-done.4.refs_4_ = bf16[2,384,768]{2,1,0:T(8,128)(2,1)S(1)} collective-permute-done((bf16[2,384,768]{2,1,0:T(8,128)(2,1)S(1)}, bf16[2,384,768]{2,1,0:T(8,128)(2,1)S(1)}, u32[]{:S(2)}, u32[]{:S(2)}) %collective-permute-start.4) | collective-permute-done | bytes 1179680 | tf_op jit(solution)/shard_map/ppermute | solution.py:17
  46.1 0.0 copy-start.3
  46.2 3.6 %collective-permute-start.7 = (bf16[384,768]{1,0:T(8,128)(2,1)S(1)}, bf16[384,768]{1,0:T(8,128)(2,1)S(1)}, u32[]{:S(2)}, u32[]{:S(2)}) collective-permute-start(bf16[384,768]{1,0:T(8,128)(2,1)S(1)} %slice_bitcast_fusion), channel_id=1, source_target_pairs={{0,96},{32,0},{64,32},{96,64},{1,97},{33,1},{65,33},{97,65},{2,98}... | collective-permute-start | bytes 1769480 | tf_op jit(solution)/shard_map/ppermute | solution.py:17
  49.8 0.0 collective-permute-done.2.refs_2_
  49.8 0.1 collective-permute-start.6
  49.9 0.0 collective-permute-done.9.refs_8_
  49.9 0.0 copy-start.5
  49.9 2.6 %collective-permute-start.13 = (bf16[2,384,768]{2,1,0:T(8,128)(2,1)S(1)}, bf16[2,384,768]{2,1,0:T(8,128)(2,1)S(1)}, u32[]{:S(2)}, u32[]{:S(2)}) collective-permute-start(bf16[2,384,768]{2,1,0:T(8,128)(2,1)S(1)} %collective-permute-done.9.refs_8_), channel_id=1, source_target_pairs={{0,96},{32,0},{64,32},{96,64},{1,97},{33,1},{65,33},{97,65},{2,98}... | collective-permute-start | bytes 3538952 | tf_op jit(solution)/shard_map/ppermute | solution.py:17
  52.6 0.0 collective-permute-start.11
  52.6 7.4 %collective-permute-done.7 = bf16[384,768]{1,0:T(8,128)(2,1)S(1)} collective-permute-done((bf16[384,768]{1,0:T(8,128)(2,1)S(1)}, bf16[384,768]{1,0:T(8,128)(2,1)S(1)}, u32[]{:S(2)}, u32[]{:S(2)}) %collective-permute-start.7) | collective-permute-done | bytes 589856 | tf_op jit(solution)/shard_map/ppermute | solution.py:17
  60.0 6.2 %collective-permute-start.10 = (bf16[2,384,768]{2,1,0:T(8,128)(2,1)S(1)}, bf16[2,384,768]{2,1,0:T(8,128)(2,1)S(1)}, u32[]{:S(2)}, u32[]{:S(2)}) collective-permute-start(bf16[2,384,768]{2,1,0:T(8,128)(2,1)S(1)} %collective-permute-done.9.refs_8_), channel_id=1, source_target_pairs={{0,16},{16,0},{1,17},{17,1},{2,18},{18,2},{3,19},{19,3},{4,20},{20... | collective-permute-start | bytes 3538952 | tf_op jit(solution)/shard_map/ppermute | solution.py:17
  66.2 0.0 collective-permute-done.6
  66.2 3.8 %collective-permute-start.5 = (bf16[2,384,768]{2,1,0:T(8,128)(2,1)S(1)}, bf16[2,384,768]{2,1,0:T(8,128)(2,1)S(1)}, u32[]{:S(2)}, u32[]{:S(2)}) collective-permute-start(bf16[2,384,768]{2,1,0:T(8,128)(2,1)S(1)} %collective-permute-done.4.refs_4_), channel_id=1, source_target_pairs={{0,16},{16,0},{1,17},{17,1},{2,18},{18,2},{3,19},{19,3},{4,20},{20... | collective-permute-start | bytes 3538952 | tf_op jit(solution)/shard_map/ppermute | solution.py:17
  70.0 0.0 copy-done.3
  70.0 0.1 pad_maximum_fusion.1.refs_6_
  70.1 0.0 copy-done.5
  70.1 0.0 copy-start.1
  70.1 0.0 collective-permute-done.1.refs_1_
  70.2 0.0 copy-start.6
  70.2 3.0 %collective-permute-start.15 = (bf16[2,384,768]{2,1,0:T(8,128)(2,1)S(1)}, bf16[2,384,768]{2,1,0:T(8,128)(2,1)S(1)}, u32[]{:S(2)}, u32[]{:S(2)}) collective-permute-start(bf16[2,384,768]{2,1,0:T(8,128)(2,1)S(1)} %pad_maximum_fusion.1.refs_6_), channel_id=1, source_target_pairs={{0,128},{128,0},{1,129},{129,1},{2,130},{130,2},{3,131},{131,3},{4... | collective-permute-start | bytes 3538952 | tf_op jit(solution)/shard_map/ppermute | solution.py:17
  73.2 12.1 %collective-permute-done.13.refs_12_ = bf16[2,384,768]{2,1,0:T(8,128)(2,1)S(1)} collective-permute-done((bf16[2,384,768]{2,1,0:T(8,128)(2,1)S(1)}, bf16[2,384,768]{2,1,0:T(8,128)(2,1)S(1)}, u32[]{:S(2)}, u32[]{:S(2)}) %collective-permute-start.13) | collective-permute-done | bytes 1179680 | tf_op jit(solution)/shard_map/ppermute | solution.py:17
  85.3 0.0 copy-done.4
  85.3 3.3 %collective-permute-start.3 = (bf16[2,384,768]{2,1,0:T(8,128)(2,1)S(1)}, bf16[2,384,768]{2,1,0:T(8,128)(2,1)S(1)}, u32[]{:S(2)}, u32[]{:S(2)}) collective-permute-start(bf16[2,384,768]{2,1,0:T(8,128)(2,1)S(1)} %collective-permute-done.2.refs_2_), channel_id=1, source_target_pairs={{0,16},{16,0},{1,17},{17,1},{2,18},{18,2},{3,19},{19,3},{4,20},{20... | collective-permute-start | bytes 3538952 | tf_op jit(solution)/shard_map/ppermute | solution.py:17
  88.6 0.1 collective-permute-done.11.refs_10_
  88.7 3.5 %collective-permute-start.8 = (bf16[2,384,768]{2,1,0:T(8,128)(2,1)S(1)}, bf16[2,384,768]{2,1,0:T(8,128)(2,1)S(1)}, u32[]{:S(2)}, u32[]{:S(2)}) collective-permute-start(bf16[2,384,768]{2,1,0:T(8,128)(2,1)S(1)} %pad_maximum_fusion.1.refs_6_), channel_id=1, source_target_pairs={{0,16},{16,0},{1,17},{17,1},{2,18},{18,2},{3,19},{19,3},{4,20},{20... | collective-permute-start | bytes 3538952 | tf_op jit(solution)/shard_map/ppermute | solution.py:17
  92.1 0.0 collective-permute-done.10.refs_9_
  92.1 0.1 collective-permute-start.14
  92.2 0.0 collective-permute-done.5.refs_5_
  92.2 0.4 collective-permute-start.12
  92.7 6.7 %collective-permute-done.15.refs_14_ = bf16[2,384,768]{2,1,0:T(8,128)(2,1)S(1)} collective-permute-done((bf16[2,384,768]{2,1,0:T(8,128)(2,1)S(1)}, bf16[2,384,768]{2,1,0:T(8,128)(2,1)S(1)}, u32[]{:S(2)}, u32[]{:S(2)}) %collective-permute-start.15) | collective-permute-done | bytes 1179680 | tf_op jit(solution)/shard_map/ppermute | solution.py:17
  99.4 0.8 collective-permute-start.16
  100.1 0.0 collective-permute-done.3.refs_3_
  100.2 0.0 collective-permute-done.8.refs_7_
  100.2 0.0 copy-done.6
  100.2 0.0 copy-start.13
  100.2 0.0 collective-permute-done.14.refs_13_
  100.2 0.0 copy-done.7
  100.2 0.0 copy-start.14
  100.2 0.0 collective-permute-done.12.refs_11_
  100.2 0.0 copy-done.8
  100.2 0.0 copy-done.9
  100.2 0.0 copy-done.10
  100.2 0.9 copy-done.12
  101.2 0.4 copy-done.13
  101.5 0.4 copy-done.14
  102.0 0.8 collective-permute-done.16.refs_15_
  102.8 0.0 copy-done.1
  102.8 0.0 copy-done.11
  102.8 0.2 copy-done.15
  103.0 14.2 %shard_map.37 = f32[512,768]{1,0:T(8,128)} custom-call(bf16[16,512,384]{2,1,0:T(8,128)(2,1)} %all-gather.2.cloned.1.call-done.tokens_ref, bf16[2,384,768]{2,1,0:T(8,128)(2,1)} %copy-done, bf16[2,384,768]{2,1,0:T(8,128)(2,1)} %copy-done.6, bf16[2,384,768]{2,1,0:T(8,128)(2,1)} %copy-done.4, bf16[2,384,768]{2,1,0:T(8,128)(2,1)} %copy-done.12, ...), custom_call_target="tpu_custom_call" | custom-call | flops 9663676416 | bytes 26738688 | tf_op jit(solution)/shard_map/pallas_call | solution.py:105
  (11 shorter events, 0.1 us)
Async XLA Ops:
  6.5 96.2 %all-gather.2.cloned.1.call-start = ((), (), s32[]{:S(2)}) async-start(), calls=%async_computation | async-start | bytes 7077888 | tf_op jit(solution)/shard_map/all_gather | solution.py:84
  6.5 1.4 %copy-start.2 = (bf16[512,384]{1,0:T(8,128)(2,1)S(1)}, bf16[512,384]{1,0:T(8,128)(2,1)}, u32[]{:S(2)}) copy-start(bf16[512,384]{1,0:T(8,128)(2,1)} %param.3) | copy-start | bytes 1179652
  8.0 17.4 %copy-start = (bf16[2,384,768]{2,1,0:T(8,128)(2,1)}, bf16[2,384,768]{2,1,0:T(8,128)(2,1)S(1)}, u32[]{:S(2)}) copy-start(bf16[2,384,768]{2,1,0:T(8,128)(2,1)S(1)} %pad_maximum_fusion.refs_0_) | copy-start | bytes 3538948
  8.0 9.8 %collective-permute-start = (bf16[512,384]{1,0:T(8,128)(2,1)S(1)}, bf16[512,384]{1,0:T(8,128)(2,1)S(1)}, u32[]{:S(2)}, u32[]{:S(2)}) collective-permute-start(bf16[512,384]{1,0:T(8,128)(2,1)S(1)} %copy-done.2), channel_id=1, source_target_pairs={{0,8},{8,0},{1,9},{9,1},{2,10},{10,2},{3,11},{11,3},{4,12},{12,4},... | collective-permute-start | bytes 1179656 | tf_op jit(solution)/shard_map/ppermute | solution.py:17
  18.8 27.4 %collective-permute-start.4 = (bf16[2,384,768]{2,1,0:T(8,128)(2,1)S(1)}, bf16[2,384,768]{2,1,0:T(8,128)(2,1)S(1)}, u32[]{:S(2)}, u32[]{:S(2)}) collective-permute-start(bf16[2,384,768]{2,1,0:T(8,128)(2,1)S(1)} %pad_maximum_fusion.refs_0_), channel_id=1, source_target_pairs={{0,96},{32,0},{64,32},{96,64},{1,97},{33,1},{65,33},{97,65},{2,98}... | collective-permute-start | bytes 3538952 | tf_op jit(solution)/shard_map/ppermute | solution.py:17
  22.4 27.4 %collective-permute-start.2 = (bf16[2,384,768]{2,1,0:T(8,128)(2,1)S(1)}, bf16[2,384,768]{2,1,0:T(8,128)(2,1)S(1)}, u32[]{:S(2)}, u32[]{:S(2)}) collective-permute-start(bf16[2,384,768]{2,1,0:T(8,128)(2,1)S(1)} %pad_maximum_fusion.refs_0_), channel_id=1, source_target_pairs={{0,32},{32,64},{64,96},{96,0},{1,33},{33,65},{65,97},{97,1},{2,34}... | collective-permute-start | bytes 3538952 | tf_op jit(solution)/shard_map/ppermute | solution.py:17
  22.4 27.5 %collective-permute-start.9 = (bf16[2,384,768]{2,1,0:T(8,128)(2,1)S(1)}, bf16[2,384,768]{2,1,0:T(8,128)(2,1)S(1)}, u32[]{:S(2)}, u32[]{:S(2)}) collective-permute-start(bf16[2,384,768]{2,1,0:T(8,128)(2,1)S(1)} %pad_maximum_fusion.refs_0_), channel_id=1, source_target_pairs={{0,128},{128,0},{1,129},{129,1},{2,130},{130,2},{3,131},{131,3},{4... | collective-permute-start | bytes 3538952 | tf_op jit(solution)/shard_map/ppermute | solution.py:17
  25.3 44.8 %collective-permute-start.1 = (bf16[2,384,768]{2,1,0:T(8,128)(2,1)S(1)}, bf16[2,384,768]{2,1,0:T(8,128)(2,1)S(1)}, u32[]{:S(2)}, u32[]{:S(2)}) collective-permute-start(bf16[2,384,768]{2,1,0:T(8,128)(2,1)S(1)} %pad_maximum_fusion.refs_0_), channel_id=1, source_target_pairs={{0,16},{16,0},{1,17},{17,1},{2,18},{18,2},{3,19},{19,3},{4,20},{20... | collective-permute-start | bytes 3538952 | tf_op jit(solution)/shard_map/ppermute | solution.py:17
  46.1 23.9 %copy-start.3 = (bf16[2,384,768]{2,1,0:T(8,128)(2,1)}, bf16[2,384,768]{2,1,0:T(8,128)(2,1)S(1)}, u32[]{:S(2)}) copy-start(bf16[2,384,768]{2,1,0:T(8,128)(2,1)S(1)} %collective-permute-done.4.refs_4_) | copy-start | bytes 3538948
  46.2 13.9 %collective-permute-start.7 = (bf16[384,768]{1,0:T(8,128)(2,1)S(1)}, bf16[384,768]{1,0:T(8,128)(2,1)S(1)}, u32[]{:S(2)}, u32[]{:S(2)}) collective-permute-start(bf16[384,768]{1,0:T(8,128)(2,1)S(1)} %slice_bitcast_fusion), channel_id=1, source_target_pairs={{0,96},{32,0},{64,32},{96,64},{1,97},{33,1},{65,33},{97,65},{2,98}... | collective-permute-start | bytes 1769480 | tf_op jit(solution)/shard_map/ppermute | solution.py:17
  49.8 35.5 %copy-start.4 = (bf16[2,384,768]{2,1,0:T(8,128)(2,1)}, bf16[2,384,768]{2,1,0:T(8,128)(2,1)S(1)}, u32[]{:S(2)}) copy-start(bf16[2,384,768]{2,1,0:T(8,128)(2,1)S(1)} %collective-permute-done.2.refs_2_) | copy-start | bytes 3538948
  49.8 16.4 %collective-permute-start.6 = (bf16[384,768]{1,0:T(8,128)(2,1)S(1)}, bf16[384,768]{1,0:T(8,128)(2,1)S(1)}, u32[]{:S(2)}, u32[]{:S(2)}) collective-permute-start(bf16[384,768]{1,0:T(8,128)(2,1)S(1)} %slice_bitcast_fusion.1), channel_id=1, source_target_pairs={{0,32},{32,64},{64,96},{96,0},{1,33},{33,65},{65,97},{97,1},{2,34}... | collective-permute-start | bytes 1769480 | tf_op jit(solution)/shard_map/ppermute | solution.py:17
  49.9 20.2 %copy-start.5 = (bf16[2,384,768]{2,1,0:T(8,128)(2,1)}, bf16[2,384,768]{2,1,0:T(8,128)(2,1)S(1)}, u32[]{:S(2)}) copy-start(bf16[2,384,768]{2,1,0:T(8,128)(2,1)S(1)} %collective-permute-done.9.refs_8_) | copy-start | bytes 3538948
  49.9 35.4 %collective-permute-start.13 = (bf16[2,384,768]{2,1,0:T(8,128)(2,1)S(1)}, bf16[2,384,768]{2,1,0:T(8,128)(2,1)S(1)}, u32[]{:S(2)}, u32[]{:S(2)}) collective-permute-start(bf16[2,384,768]{2,1,0:T(8,128)(2,1)S(1)} %collective-permute-done.9.refs_8_), channel_id=1, source_target_pairs={{0,96},{32,0},{64,32},{96,64},{1,97},{33,1},{65,33},{97,65},{2,98}... | collective-permute-start | bytes 3538952 | tf_op jit(solution)/shard_map/ppermute | solution.py:17
  52.6 36.1 %collective-permute-start.11 = (bf16[2,384,768]{2,1,0:T(8,128)(2,1)S(1)}, bf16[2,384,768]{2,1,0:T(8,128)(2,1)S(1)}, u32[]{:S(2)}, u32[]{:S(2)}) collective-permute-start(bf16[2,384,768]{2,1,0:T(8,128)(2,1)S(1)} %collective-permute-done.9.refs_8_), channel_id=1, source_target_pairs={{0,32},{32,64},{64,96},{96,0},{1,33},{33,65},{65,97},{97,1},{2,34}... | collective-permute-start | bytes 3538952 | tf_op jit(solution)/shard_map/ppermute | solution.py:17
  60.0 32.1 %collective-permute-start.10 = (bf16[2,384,768]{2,1,0:T(8,128)(2,1)S(1)}, bf16[2,384,768]{2,1,0:T(8,128)(2,1)S(1)}, u32[]{:S(2)}, u32[]{:S(2)}) collective-permute-start(bf16[2,384,768]{2,1,0:T(8,128)(2,1)S(1)} %collective-permute-done.9.refs_8_), channel_id=1, source_target_pairs={{0,16},{16,0},{1,17},{17,1},{2,18},{18,2},{3,19},{19,3},{4,20},{20... | collective-permute-start | bytes 3538952 | tf_op jit(solution)/shard_map/ppermute | solution.py:17
  66.2 26.0 %collective-permute-start.5 = (bf16[2,384,768]{2,1,0:T(8,128)(2,1)S(1)}, bf16[2,384,768]{2,1,0:T(8,128)(2,1)S(1)}, u32[]{:S(2)}, u32[]{:S(2)}) collective-permute-start(bf16[2,384,768]{2,1,0:T(8,128)(2,1)S(1)} %collective-permute-done.4.refs_4_), channel_id=1, source_target_pairs={{0,16},{16,0},{1,17},{17,1},{2,18},{18,2},{3,19},{19,3},{4,20},{20... | collective-permute-start | bytes 3538952 | tf_op jit(solution)/shard_map/ppermute | solution.py:17
  70.1 32.6 %copy-start.1 = (bf16[2,384,768]{2,1,0:T(8,128)(2,1)}, bf16[2,384,768]{2,1,0:T(8,128)(2,1)S(1)}, u32[]{:S(2)}) copy-start(bf16[2,384,768]{2,1,0:T(8,128)(2,1)S(1)} %pad_maximum_fusion.1.refs_6_) | copy-start | bytes 3538948
  70.2 30.0 %copy-start.6 = (bf16[2,384,768]{2,1,0:T(8,128)(2,1)}, bf16[2,384,768]{2,1,0:T(8,128)(2,1)S(1)}, u32[]{:S(2)}) copy-start(bf16[2,384,768]{2,1,0:T(8,128)(2,1)S(1)} %collective-permute-done.1.refs_1_) | copy-start | bytes 3538948
  70.2 29.2 %collective-permute-start.15 = (bf16[2,384,768]{2,1,0:T(8,128)(2,1)S(1)}, bf16[2,384,768]{2,1,0:T(8,128)(2,1)S(1)}, u32[]{:S(2)}, u32[]{:S(2)}) collective-permute-start(bf16[2,384,768]{2,1,0:T(8,128)(2,1)S(1)} %pad_maximum_fusion.1.refs_6_), channel_id=1, source_target_pairs={{0,128},{128,0},{1,129},{129,1},{2,130},{130,2},{3,131},{131,3},{4... | collective-permute-start | bytes 3538952 | tf_op jit(solution)/shard_map/ppermute | solution.py:17
  85.3 14.9 %copy-start.7 = (bf16[2,384,768]{2,1,0:T(8,128)(2,1)}, bf16[2,384,768]{2,1,0:T(8,128)(2,1)S(1)}, u32[]{:S(2)}) copy-start(bf16[2,384,768]{2,1,0:T(8,128)(2,1)S(1)} %collective-permute-done.13.refs_12_) | copy-start | bytes 3538948
  85.3 14.8 %collective-permute-start.3 = (bf16[2,384,768]{2,1,0:T(8,128)(2,1)S(1)}, bf16[2,384,768]{2,1,0:T(8,128)(2,1)S(1)}, u32[]{:S(2)}, u32[]{:S(2)}) collective-permute-start(bf16[2,384,768]{2,1,0:T(8,128)(2,1)S(1)} %collective-permute-done.2.refs_2_), channel_id=1, source_target_pairs={{0,16},{16,0},{1,17},{17,1},{2,18},{18,2},{3,19},{19,3},{4,20},{20... | collective-permute-start | bytes 3538952 | tf_op jit(solution)/shard_map/ppermute | solution.py:17
  88.7 11.6 %copy-start.8 = (bf16[2,384,768]{2,1,0:T(8,128)(2,1)}, bf16[2,384,768]{2,1,0:T(8,128)(2,1)S(1)}, u32[]{:S(2)}) copy-start(bf16[2,384,768]{2,1,0:T(8,128)(2,1)S(1)} %collective-permute-done.11.refs_10_) | copy-start | bytes 3538948
  88.7 11.5 %collective-permute-start.8 = (bf16[2,384,768]{2,1,0:T(8,128)(2,1)S(1)}, bf16[2,384,768]{2,1,0:T(8,128)(2,1)S(1)}, u32[]{:S(2)}, u32[]{:S(2)}) collective-permute-start(bf16[2,384,768]{2,1,0:T(8,128)(2,1)S(1)} %pad_maximum_fusion.1.refs_6_), channel_id=1, source_target_pairs={{0,16},{16,0},{1,17},{17,1},{2,18},{18,2},{3,19},{19,3},{4,20},{20... | collective-permute-start | bytes 3538952 | tf_op jit(solution)/shard_map/ppermute | solution.py:17
  92.1 8.1 %copy-start.9 = (bf16[2,384,768]{2,1,0:T(8,128)(2,1)}, bf16[2,384,768]{2,1,0:T(8,128)(2,1)S(1)}, u32[]{:S(2)}) copy-start(bf16[2,384,768]{2,1,0:T(8,128)(2,1)S(1)} %collective-permute-done.10.refs_9_) | copy-start | bytes 3538948
  92.1 8.0 %collective-permute-start.14 = (bf16[2,384,768]{2,1,0:T(8,128)(2,1)S(1)}, bf16[2,384,768]{2,1,0:T(8,128)(2,1)S(1)}, u32[]{:S(2)}, u32[]{:S(2)}) collective-permute-start(bf16[2,384,768]{2,1,0:T(8,128)(2,1)S(1)} %collective-permute-done.13.refs_12_), channel_id=1, source_target_pairs={{0,16},{16,0},{1,17},{17,1},{2,18},{18,2},{3,19},{19,3},{4,20},{20... | collective-permute-start | bytes 3538952 | tf_op jit(solution)/shard_map/ppermute | solution.py:17
  92.2 8.0 %copy-start.10 = (bf16[2,384,768]{2,1,0:T(8,128)(2,1)}, bf16[2,384,768]{2,1,0:T(8,128)(2,1)S(1)}, u32[]{:S(2)}) copy-start(bf16[2,384,768]{2,1,0:T(8,128)(2,1)S(1)} %collective-permute-done.5.refs_5_) | copy-start | bytes 3538948
  92.2 8.0 %collective-permute-start.12 = (bf16[2,384,768]{2,1,0:T(8,128)(2,1)S(1)}, bf16[2,384,768]{2,1,0:T(8,128)(2,1)S(1)}, u32[]{:S(2)}, u32[]{:S(2)}) collective-permute-start(bf16[2,384,768]{2,1,0:T(8,128)(2,1)S(1)} %collective-permute-done.11.refs_10_), channel_id=1, source_target_pairs={{0,16},{16,0},{1,17},{17,1},{2,18},{18,2},{3,19},{19,3},{4,20},{20... | collective-permute-start | bytes 3538952 | tf_op jit(solution)/shard_map/ppermute | solution.py:17
  99.4 3.4 %copy-start.11 = (bf16[2,384,768]{2,1,0:T(8,128)(2,1)}, bf16[2,384,768]{2,1,0:T(8,128)(2,1)S(1)}, u32[]{:S(2)}) copy-start(bf16[2,384,768]{2,1,0:T(8,128)(2,1)S(1)} %collective-permute-done.15.refs_14_) | copy-start | bytes 3538948
  99.4 3.4 %collective-permute-start.16 = (bf16[2,384,768]{2,1,0:T(8,128)(2,1)S(1)}, bf16[2,384,768]{2,1,0:T(8,128)(2,1)}, u32[]{:S(2)}, u32[]{:S(2)}) collective-permute-start(bf16[2,384,768]{2,1,0:T(8,128)(2,1)S(1)} %collective-permute-done.15.refs_14_), channel_id=1, source_target_pairs={{0,16},{16,0},{1,17},{17,1},{2,18},{18,2},{3,19},{19,3},{4,20},{20... | collective-permute-start | bytes 3538952 | tf_op jit(solution)/shard_map/ppermute | solution.py:17
  100.2 1.0 copy-start.12
  100.2 1.4 %copy-start.13 = (bf16[2,384,768]{2,1,0:T(8,128)(2,1)}, bf16[2,384,768]{2,1,0:T(8,128)(2,1)S(1)}, u32[]{:S(2)}) copy-start(bf16[2,384,768]{2,1,0:T(8,128)(2,1)S(1)} %collective-permute-done.8.refs_7_) | copy-start | bytes 3538948
  100.2 1.8 %copy-start.14 = (bf16[2,384,768]{2,1,0:T(8,128)(2,1)}, bf16[2,384,768]{2,1,0:T(8,128)(2,1)S(1)}, u32[]{:S(2)}) copy-start(bf16[2,384,768]{2,1,0:T(8,128)(2,1)S(1)} %collective-permute-done.14.refs_13_) | copy-start | bytes 3538948
  102.0 1.0 copy-start.15
Sparse Core Ops, SparseCore 0:
  18.9 79.4 all-gather.1

commit v3 on v2

--- a/solution.py
+++ b/solution.py
@@ -15,6 +15,11 @@
 
 def shift(value, axis, size, by):
     return lax.ppermute(value, axis, [(i, (i + by) % size) for i in range(size)])
+
+
+def after(waits, *values):
+    waits, values = lax.optimization_barrier((tuple(waits), tuple(values)))
+    return values
 
 
 def multiply(origins, tokens_ref, *refs):
@@ -82,8 +87,9 @@
     own_2 = jnp.stack([own_2g, own_2u])
     pair = jnp.stack([tokens, other_tokens])
     gathered = lax.all_gather(pair, "z", axis=0, tiled=True)
-    across_1 = shift(across, "x", 4, 1)
-    across_3 = shift(across, "x", 4, -1)
+    (across_late,) = after([own_2g, own_2u], across)
+    across_1 = shift(across_late, "x", 4, 1)
+    across_3 = shift(across_late, "x", 4, -1)
     across_2 = shift(own_2, "y_hi", 2, 1)
 
     blocks = [

time: 124 us -> 121 us (0.976)
  starting transfers between devices: 38.2 us -> 33.7 us
  waiting for transfers between devices: 53.5 us -> 55.3 us
    ppermute x17, starting transfers between devices: 38.2 us -> 33.7 us  [shift(): lax.ppermute(value, axis, [(i, (i + by) % size) for i in range(size)])]
    ppermute x17, waiting for transfers between devices: 53.4 us -> 55.3 us  [shift(): lax.ppermute(value, axis, [(i, (i + by) % size) for i in range(size)])]
where the time goes in v3:
time: 121 us
  waiting for transfers between devices  55.3 us (46%)
  starting transfers between devices  33.7 us (28%)
  Pallas kernels  14.2 us (12%)
  between operations  13.5 us (11%)
  other arithmetic  2.48 us (2%)
  local copies, waits for them, and re-layouts  1.35 us (1%)
    ppermute x17, waiting for transfers between devices, shift(): lax.ppermute(value, axis, [(i, (i + by) % size) for i in range(size)])  55.3 us
    ppermute x17, starting transfers between devices, shift(): lax.ppermute(value, axis, [(i, (i + by) % size) for i in range(size)])  33.7 us
    pallas_call x1, Pallas kernels, per_device(): pl.pallas_call(functools.partial(multiply, origins), out_shape=jax.ShapeD...  14.2 us
  transfers between devices with their start and end apart: 18, of which 7 were waited for; matrix products, arithmetic and copies ran while one was open for 0% of the time, Pallas kernels for 0%

profile of v3, /device:TPU:1, one launch (start us, length us, event | category | flops | bytes accessed | tf_op | source)
XLA Modules:
  0.0 120.6 jit_solution(6495429024199458467)
XLA Ops:
  6.5 0.0 all-gather.2.cloned.1.call-start
  6.5 0.0 copy-start.2
  6.5 1.4 %pad_maximum_fusion.refs_0_ = bf16[2,384,768]{2,1,0:T(8,128)(2,1)S(1)} fusion(bf16[1,384,768]{2,1,0:T(8,128)(2,1)} %bitcast.10, bf16[1,384,768]{2,1,0:T(8,128)(2,1)} %bitcast.11), kind=kLoop, calls=%fused_computation | loop fusion | flops 589824 | bytes 2359296 | tf_op jit(solution)/shard_map/stack | solution.py:79
  7.9 0.0 copy-done.2
  8.0 0.0 copy-start
  8.0 2.2 %collective-permute-start = (bf16[512,384]{1,0:T(8,128)(2,1)S(1)}, bf16[512,384]{1,0:T(8,128)(2,1)S(1)}, u32[]{:S(2)}, u32[]{:S(2)}) collective-permute-start(bf16[512,384]{1,0:T(8,128)(2,1)S(1)} %copy-done.2), channel_id=1, source_target_pairs={{0,8},{8,0},{1,9},{9,1},{2,10},{10,2},{3,11},{11,3},{4,12},{12,4},... | collective-permute-start | bytes 1179656 | tf_op jit(solution)/shard_map/ppermute | solution.py:17
  10.2 7.6 %collective-permute-done = bf16[512,384]{1,0:T(8,128)(2,1)S(1)} collective-permute-done((bf16[512,384]{1,0:T(8,128)(2,1)S(1)}, bf16[512,384]{1,0:T(8,128)(2,1)S(1)}, u32[]{:S(2)}, u32[]{:S(2)}) %collective-permute-start) | collective-permute-done | bytes 393248 | tf_op jit(solution)/shard_map/ppermute | solution.py:17
  17.8 1.0 pad_maximum_fusion.2
  18.7 0.0 all-gather.2.cloned.1.call-update
  18.8 3.7 %collective-permute-start.4 = (bf16[2,384,768]{2,1,0:T(8,128)(2,1)S(1)}, bf16[2,384,768]{2,1,0:T(8,128)(2,1)S(1)}, u32[]{:S(2)}, u32[]{:S(2)}) collective-permute-start(bf16[2,384,768]{2,1,0:T(8,128)(2,1)S(1)} %pad_maximum_fusion.refs_0_), channel_id=1, source_target_pairs={{0,96},{32,0},{64,32},{96,64},{1,97},{33,1},{65,33},{97,65},{2,98}... | collective-permute-start | bytes 3538952 | tf_op jit(solution)/shard_map/ppermute | solution.py:17
  22.4 0.0 collective-permute-start.2
  22.4 2.9 %collective-permute-start.9 = (bf16[2,384,768]{2,1,0:T(8,128)(2,1)S(1)}, bf16[2,384,768]{2,1,0:T(8,128)(2,1)S(1)}, u32[]{:S(2)}, u32[]{:S(2)}) collective-permute-start(bf16[2,384,768]{2,1,0:T(8,128)(2,1)S(1)} %pad_maximum_fusion.refs_0_), channel_id=1, source_target_pairs={{0,128},{128,0},{1,129},{129,1},{2,130},{130,2},{3,131},{131,3},{4... | collective-permute-start | bytes 3538952 | tf_op jit(solution)/shard_map/ppermute | solution.py:17
  25.3 0.0 copy-done
  25.3 2.1 %collective-permute-start.1 = (bf16[2,384,768]{2,1,0:T(8,128)(2,1)S(1)}, bf16[2,384,768]{2,1,0:T(8,128)(2,1)S(1)}, u32[]{:S(2)}, u32[]{:S(2)}) collective-permute-start(bf16[2,384,768]{2,1,0:T(8,128)(2,1)S(1)} %pad_maximum_fusion.refs_0_), channel_id=1, source_target_pairs={{0,16},{16,0},{1,17},{17,1},{2,18},{18,2},{3,19},{19,3},{4,20},{20... | collective-permute-start | bytes 3538952 | tf_op jit(solution)/shard_map/ppermute | solution.py:17
  27.4 18.7 %collective-permute-done.4.refs_4_ = bf16[2,384,768]{2,1,0:T(8,128)(2,1)S(1)} collective-permute-done((bf16[2,384,768]{2,1,0:T(8,128)(2,1)S(1)}, bf16[2,384,768]{2,1,0:T(8,128)(2,1)S(1)}, u32[]{:S(2)}, u32[]{:S(2)}) %collective-permute-start.4) | collective-permute-done | bytes 1179680 | tf_op jit(solution)/shard_map/ppermute | solution.py:17
  46.1 0.0 copy-start.3
  46.2 3.6 %collective-permute-start.7 = (bf16[384,768]{1,0:T(8,128)(2,1)S(1)}, bf16[384,768]{1,0:T(8,128)(2,1)S(1)}, u32[]{:S(2)}, u32[]{:S(2)}) collective-permute-start(bf16[384,768]{1,0:T(8,128)(2,1)S(1)} %slice_bitcast_fusion), channel_id=1, source_target_pairs={{0,96},{32,0},{64,32},{96,64},{1,97},{33,1},{65,33},{97,65},{2,98}... | collective-permute-start | bytes 1769480 | tf_op jit(solution)/shard_map/ppermute | solution.py:17
  49.8 0.0 collective-permute-done.2.refs_2_
  49.8 0.0 copy-start.4
  49.8 0.1 collective-permute-start.6
  49.9 2.7 %collective-permute-start.5 = (bf16[2,384,768]{2,1,0:T(8,128)(2,1)S(1)}, bf16[2,384,768]{2,1,0:T(8,128)(2,1)S(1)}, u32[]{:S(2)}, u32[]{:S(2)}) collective-permute-start(bf16[2,384,768]{2,1,0:T(8,128)(2,1)S(1)} %collective-permute-done.4.refs_4_), channel_id=1, source_target_pairs={{0,16},{16,0},{1,17},{17,1},{2,18},{18,2},{3,19},{19,3},{4,20},{20... | collective-permute-start | bytes 3538952 | tf_op jit(solution)/shard_map/ppermute | solution.py:17
  52.6 0.0 collective-permute-done.9.refs_8_
  52.6 0.0 copy-start.5
  52.6 0.1 collective-permute-start.10
  52.8 7.3 %collective-permute-done.7 = bf16[384,768]{1,0:T(8,128)(2,1)S(1)} collective-permute-done((bf16[384,768]{1,0:T(8,128)(2,1)S(1)}, bf16[384,768]{1,0:T(8,128)(2,1)S(1)}, u32[]{:S(2)}, u32[]{:S(2)}) %collective-permute-start.7) | collective-permute-done | bytes 589856 | tf_op jit(solution)/shard_map/ppermute | solution.py:17
  60.0 3.4 %collective-permute-done.6 = bf16[384,768]{1,0:T(8,128)(2,1)S(1)} collective-permute-done((bf16[384,768]{1,0:T(8,128)(2,1)S(1)}, bf16[384,768]{1,0:T(8,128)(2,1)S(1)}, u32[]{:S(2)}, u32[]{:S(2)}) %collective-permute-start.6) | collective-permute-done | bytes 589856 | tf_op jit(solution)/shard_map/ppermute | solution.py:17
  63.4 0.0 copy-done.3
  63.4 0.1 pad_maximum_fusion.1.refs_6_
  63.5 0.0 copy-start.1
  63.5 3.0 %collective-permute-start.15 = (bf16[2,384,768]{2,1,0:T(8,128)(2,1)S(1)}, bf16[2,384,768]{2,1,0:T(8,128)(2,1)S(1)}, u32[]{:S(2)}, u32[]{:S(2)}) collective-permute-start(bf16[2,384,768]{2,1,0:T(8,128)(2,1)S(1)} %pad_maximum_fusion.1.refs_6_), channel_id=1, source_target_pairs={{0,128},{128,0},{1,129},{129,1},{2,130},{130,2},{3,131},{131,3},{4... | collective-permute-start | bytes 3538952 | tf_op jit(solution)/shard_map/ppermute | solution.py:17
  66.5 0.2 collective-permute-start.13
  66.7 0.0 collective-permute-done.1.refs_1_
  66.7 0.0 copy-done.5
  66.7 1.4 %collective-permute-start.11 = (bf16[2,384,768]{2,1,0:T(8,128)(2,1)S(1)}, bf16[2,384,768]{2,1,0:T(8,128)(2,1)S(1)}, u32[]{:S(2)}, u32[]{:S(2)}) collective-permute-start(bf16[2,384,768]{2,1,0:T(8,128)(2,1)S(1)} %collective-permute-done.9.refs_8_), channel_id=1, source_target_pairs={{0,32},{32,64},{64,96},{96,0},{1,33},{33,65},{65,97},{97,1},{2,34}... | collective-permute-start | bytes 3538952 | tf_op jit(solution)/shard_map/ppermute | solution.py:17
  68.1 0.0 collective-permute-done.10.refs_9_
  68.1 0.0 copy-done.4
  68.1 4.4 %collective-permute-start.3 = (bf16[2,384,768]{2,1,0:T(8,128)(2,1)S(1)}, bf16[2,384,768]{2,1,0:T(8,128)(2,1)S(1)}, u32[]{:S(2)}, u32[]{:S(2)}) collective-permute-start(bf16[2,384,768]{2,1,0:T(8,128)(2,1)S(1)} %collective-permute-done.2.refs_2_), channel_id=1, source_target_pairs={{0,16},{16,0},{1,17},{17,1},{2,18},{18,2},{3,19},{19,3},{4,20},{20... | collective-permute-start | bytes 3538952 | tf_op jit(solution)/shard_map/ppermute | solution.py:17
  72.5 0.0 collective-permute-done.5.refs_5_
  72.5 0.1 collective-permute-start.8
  72.6 16.5 %collective-permute-done.15.refs_14_ = bf16[2,384,768]{2,1,0:T(8,128)(2,1)S(1)} collective-permute-done((bf16[2,384,768]{2,1,0:T(8,128)(2,1)S(1)}, bf16[2,384,768]{2,1,0:T(8,128)(2,1)S(1)}, u32[]{:S(2)}, u32[]{:S(2)}) %collective-permute-start.15) | collective-permute-done | bytes 1179680 | tf_op jit(solution)/shard_map/ppermute | solution.py:17
  89.1 4.4 %collective-permute-start.16 = (bf16[2,384,768]{2,1,0:T(8,128)(2,1)S(1)}, bf16[2,384,768]{2,1,0:T(8,128)(2,1)S(1)}, u32[]{:S(2)}, u32[]{:S(2)}) collective-permute-start(bf16[2,384,768]{2,1,0:T(8,128)(2,1)S(1)} %collective-permute-done.15.refs_14_), channel_id=1, source_target_pairs={{0,16},{16,0},{1,17},{17,1},{2,18},{18,2},{3,19},{19,3},{4,20},{20... | collective-permute-start | bytes 3538952 | tf_op jit(solution)/shard_map/ppermute | solution.py:17
  93.5 0.0 collective-permute-done.13.refs_12_
  93.5 1.4 %collective-permute-start.14 = (bf16[2,384,768]{2,1,0:T(8,128)(2,1)S(1)}, bf16[2,384,768]{2,1,0:T(8,128)(2,1)S(1)}, u32[]{:S(2)}, u32[]{:S(2)}) collective-permute-start(bf16[2,384,768]{2,1,0:T(8,128)(2,1)S(1)} %collective-permute-done.13.refs_12_), channel_id=1, source_target_pairs={{0,16},{16,0},{1,17},{17,1},{2,18},{18,2},{3,19},{19,3},{4,20},{20... | collective-permute-start | bytes 3538952 | tf_op jit(solution)/shard_map/ppermute | solution.py:17
  94.9 0.0 collective-permute-done.11.refs_10_
  94.9 1.4 %collective-permute-start.12 = (bf16[2,384,768]{2,1,0:T(8,128)(2,1)S(1)}, bf16[2,384,768]{2,1,0:T(8,128)(2,1)}, u32[]{:S(2)}, u32[]{:S(2)}) collective-permute-start(bf16[2,384,768]{2,1,0:T(8,128)(2,1)S(1)} %collective-permute-done.11.refs_10_), channel_id=1, source_target_pairs={{0,16},{16,0},{1,17},{17,1},{2,18},{18,2},{3,19},{19,3},{4,20},{20... | collective-permute-start | bytes 3538952 | tf_op jit(solution)/shard_map/ppermute | solution.py:17
  96.4 0.0 collective-permute-done.3.refs_3_
  96.4 0.0 collective-permute-done.8.refs_7_
  96.4 0.0 copy-done.6
  96.4 0.0 copy-start.13
  96.4 0.0 collective-permute-done.16.refs_15_
  96.4 0.0 copy-done.7
  96.4 0.0 copy-start.14
  96.4 1.2 %collective-permute-done.14.refs_13_ = bf16[2,384,768]{2,1,0:T(8,128)(2,1)S(1)} collective-permute-done((bf16[2,384,768]{2,1,0:T(8,128)(2,1)S(1)}, bf16[2,384,768]{2,1,0:T(8,128)(2,1)S(1)}, u32[]{:S(2)}, u32[]{:S(2)}) %collective-permute-start.14) | collective-permute-done | bytes 1179680 | tf_op jit(solution)/shard_map/ppermute | solution.py:17
  97.7 0.0 copy-done.8
  97.7 0.0 copy-done.9
  97.7 0.0 copy-done.10
  97.7 0.0 copy-done.12
  97.7 0.2 copy-done.14
  97.8 1.1 copy-done.15
  98.9 0.6 collective-permute-done.12.refs_11_
  99.5 0.0 copy-done.1
  99.5 0.0 copy-done.11
  99.5 0.0 copy-done.13
  99.5 14.2 %shard_map.37 = f32[512,768]{1,0:T(8,128)} custom-call(bf16[16,512,384]{2,1,0:T(8,128)(2,1)} %all-gather.2.cloned.1.call-done.tokens_ref, bf16[2,384,768]{2,1,0:T(8,128)(2,1)} %copy-done, bf16[2,384,768]{2,1,0:T(8,128)(2,1)} %copy-done.6, bf16[2,384,768]{2,1,0:T(8,128)(2,1)} %copy-done.4, bf16[2,384,768]{2,1,0:T(8,128)(2,1)} %copy-done.12, ...), custom_call_target="tpu_custom_call" | custom-call | flops 9663676416 | bytes 26738688 | tf_op jit(solution)/shard_map/pallas_call | solution.py:111
  (11 shorter events, 0.1 us)
Async XLA Ops:
  6.5 92.9 %all-gather.2.cloned.1.call-start = ((), (), s32[]{:S(2)}) async-start(), calls=%async_computation | async-start | bytes 7077888 | tf_op jit(solution)/shard_map/all_gather | solution.py:89
  6.5 1.4 %copy-start.2 = (bf16[512,384]{1,0:T(8,128)(2,1)S(1)}, bf16[512,384]{1,0:T(8,128)(2,1)}, u32[]{:S(2)}) copy-start(bf16[512,384]{1,0:T(8,128)(2,1)} %param.3) | copy-start | bytes 1179652
  8.0 17.4 %copy-start = (bf16[2,384,768]{2,1,0:T(8,128)(2,1)}, bf16[2,384,768]{2,1,0:T(8,128)(2,1)S(1)}, u32[]{:S(2)}) copy-start(bf16[2,384,768]{2,1,0:T(8,128)(2,1)S(1)} %pad_maximum_fusion.refs_0_) | copy-start | bytes 3538948
  8.0 9.8 %collective-permute-start = (bf16[512,384]{1,0:T(8,128)(2,1)S(1)}, bf16[512,384]{1,0:T(8,128)(2,1)S(1)}, u32[]{:S(2)}, u32[]{:S(2)}) collective-permute-start(bf16[512,384]{1,0:T(8,128)(2,1)S(1)} %copy-done.2), channel_id=1, source_target_pairs={{0,8},{8,0},{1,9},{9,1},{2,10},{10,2},{3,11},{11,3},{4,12},{12,4},... | collective-permute-start | bytes 1179656 | tf_op jit(solution)/shard_map/ppermute | solution.py:17
  18.8 27.4 %collective-permute-start.4 = (bf16[2,384,768]{2,1,0:T(8,128)(2,1)S(1)}, bf16[2,384,768]{2,1,0:T(8,128)(2,1)S(1)}, u32[]{:S(2)}, u32[]{:S(2)}) collective-permute-start(bf16[2,384,768]{2,1,0:T(8,128)(2,1)S(1)} %pad_maximum_fusion.refs_0_), channel_id=1, source_target_pairs={{0,96},{32,0},{64,32},{96,64},{1,97},{33,1},{65,33},{97,65},{2,98}... | collective-permute-start | bytes 3538952 | tf_op jit(solution)/shard_map/ppermute | solution.py:17
  22.4 27.4 %collective-permute-start.2 = (bf16[2,384,768]{2,1,0:T(8,128)(2,1)S(1)}, bf16[2,384,768]{2,1,0:T(8,128)(2,1)S(1)}, u32[]{:S(2)}, u32[]{:S(2)}) collective-permute-start(bf16[2,384,768]{2,1,0:T(8,128)(2,1)S(1)} %pad_maximum_fusion.refs_0_), channel_id=1, source_target_pairs={{0,32},{32,64},{64,96},{96,0},{1,33},{33,65},{65,97},{97,1},{2,34}... | collective-permute-start | bytes 3538952 | tf_op jit(solution)/shard_map/ppermute | solution.py:17
  22.4 30.2 %collective-permute-start.9 = (bf16[2,384,768]{2,1,0:T(8,128)(2,1)S(1)}, bf16[2,384,768]{2,1,0:T(8,128)(2,1)S(1)}, u32[]{:S(2)}, u32[]{:S(2)}) collective-permute-start(bf16[2,384,768]{2,1,0:T(8,128)(2,1)S(1)} %pad_maximum_fusion.refs_0_), channel_id=1, source_target_pairs={{0,128},{128,0},{1,129},{129,1},{2,130},{130,2},{3,131},{131,3},{4... | collective-permute-start | bytes 3538952 | tf_op jit(solution)/shard_map/ppermute | solution.py:17
  25.3 41.3 %collective-permute-start.1 = (bf16[2,384,768]{2,1,0:T(8,128)(2,1)S(1)}, bf16[2,384,768]{2,1,0:T(8,128)(2,1)S(1)}, u32[]{:S(2)}, u32[]{:S(2)}) collective-permute-start(bf16[2,384,768]{2,1,0:T(8,128)(2,1)S(1)} %pad_maximum_fusion.refs_0_), channel_id=1, source_target_pairs={{0,16},{16,0},{1,17},{17,1},{2,18},{18,2},{3,19},{19,3},{4,20},{20... | collective-permute-start | bytes 3538952 | tf_op jit(solution)/shard_map/ppermute | solution.py:17
  46.1 17.3 %copy-start.3 = (bf16[2,384,768]{2,1,0:T(8,128)(2,1)}, bf16[2,384,768]{2,1,0:T(8,128)(2,1)S(1)}, u32[]{:S(2)}) copy-start(bf16[2,384,768]{2,1,0:T(8,128)(2,1)S(1)} %collective-permute-done.4.refs_4_) | copy-start | bytes 3538948
  46.2 13.9 %collective-permute-start.7 = (bf16[384,768]{1,0:T(8,128)(2,1)S(1)}, bf16[384,768]{1,0:T(8,128)(2,1)S(1)}, u32[]{:S(2)}, u32[]{:S(2)}) collective-permute-start(bf16[384,768]{1,0:T(8,128)(2,1)S(1)} %slice_bitcast_fusion), channel_id=1, source_target_pairs={{0,96},{32,0},{64,32},{96,64},{1,97},{33,1},{65,33},{97,65},{2,98}... | collective-permute-start | bytes 1769480 | tf_op jit(solution)/shard_map/ppermute | solution.py:17
  49.8 18.3 %copy-start.4 = (bf16[2,384,768]{2,1,0:T(8,128)(2,1)}, bf16[2,384,768]{2,1,0:T(8,128)(2,1)S(1)}, u32[]{:S(2)}) copy-start(bf16[2,384,768]{2,1,0:T(8,128)(2,1)S(1)} %collective-permute-done.2.refs_2_) | copy-start | bytes 3538948
  49.8 13.6 %collective-permute-start.6 = (bf16[384,768]{1,0:T(8,128)(2,1)S(1)}, bf16[384,768]{1,0:T(8,128)(2,1)S(1)}, u32[]{:S(2)}, u32[]{:S(2)}) collective-permute-start(bf16[384,768]{1,0:T(8,128)(2,1)S(1)} %slice_bitcast_fusion.1), channel_id=1, source_target_pairs={{0,32},{32,64},{64,96},{96,0},{1,33},{33,65},{65,97},{97,1},{2,34}... | collective-permute-start | bytes 1769480 | tf_op jit(solution)/shard_map/ppermute | solution.py:17
  49.9 22.5 %collective-permute-start.5 = (bf16[2,384,768]{2,1,0:T(8,128)(2,1)S(1)}, bf16[2,384,768]{2,1,0:T(8,128)(2,1)S(1)}, u32[]{:S(2)}, u32[]{:S(2)}) collective-permute-start(bf16[2,384,768]{2,1,0:T(8,128)(2,1)S(1)} %collective-permute-done.4.refs_4_), channel_id=1, source_target_pairs={{0,16},{16,0},{1,17},{17,1},{2,18},{18,2},{3,19},{19,3},{4,20},{20... | collective-permute-start | bytes 3538952 | tf_op jit(solution)/shard_map/ppermute | solution.py:17
  52.6 14.0 %copy-start.5 = (bf16[2,384,768]{2,1,0:T(8,128)(2,1)}, bf16[2,384,768]{2,1,0:T(8,128)(2,1)S(1)}, u32[]{:S(2)}) copy-start(bf16[2,384,768]{2,1,0:T(8,128)(2,1)S(1)} %collective-permute-done.9.refs_8_) | copy-start | bytes 3538948
  52.6 15.4 %collective-permute-start.10 = (bf16[2,384,768]{2,1,0:T(8,128)(2,1)S(1)}, bf16[2,384,768]{2,1,0:T(8,128)(2,1)S(1)}, u32[]{:S(2)}, u32[]{:S(2)}) collective-permute-start(bf16[2,384,768]{2,1,0:T(8,128)(2,1)S(1)} %collective-permute-done.9.refs_8_), channel_id=1, source_target_pairs={{0,16},{16,0},{1,17},{17,1},{2,18},{18,2},{3,19},{19,3},{4,20},{20... | collective-permute-start | bytes 3538952 | tf_op jit(solution)/shard_map/ppermute | solution.py:17
  63.5 36.0 %copy-start.1 = (bf16[2,384,768]{2,1,0:T(8,128)(2,1)}, bf16[2,384,768]{2,1,0:T(8,128)(2,1)S(1)}, u32[]{:S(2)}) copy-start(bf16[2,384,768]{2,1,0:T(8,128)(2,1)S(1)} %pad_maximum_fusion.1.refs_6_) | copy-start | bytes 3538948
  63.5 25.6 %collective-permute-start.15 = (bf16[2,384,768]{2,1,0:T(8,128)(2,1)S(1)}, bf16[2,384,768]{2,1,0:T(8,128)(2,1)S(1)}, u32[]{:S(2)}, u32[]{:S(2)}) collective-permute-start(bf16[2,384,768]{2,1,0:T(8,128)(2,1)S(1)} %pad_maximum_fusion.1.refs_6_), channel_id=1, source_target_pairs={{0,128},{128,0},{1,129},{129,1},{2,130},{130,2},{3,131},{131,3},{4... | collective-permute-start | bytes 3538952 | tf_op jit(solution)/shard_map/ppermute | solution.py:17
  66.5 27.0 %collective-permute-start.13 = (bf16[2,384,768]{2,1,0:T(8,128)(2,1)S(1)}, bf16[2,384,768]{2,1,0:T(8,128)(2,1)S(1)}, u32[]{:S(2)}, u32[]{:S(2)}) collective-permute-start(bf16[2,384,768]{2,1,0:T(8,128)(2,1)S(1)} %collective-permute-done.9.refs_8_), channel_id=1, source_target_pairs={{0,96},{32,0},{64,32},{96,64},{1,97},{33,1},{65,33},{97,65},{2,98}... | collective-permute-start | bytes 3538952 | tf_op jit(solution)/shard_map/ppermute | solution.py:17
  66.7 29.7 %copy-start.6 = (bf16[2,384,768]{2,1,0:T(8,128)(2,1)}, bf16[2,384,768]{2,1,0:T(8,128)(2,1)S(1)}, u32[]{:S(2)}) copy-start(bf16[2,384,768]{2,1,0:T(8,128)(2,1)S(1)} %collective-permute-done.1.refs_1_) | copy-start | bytes 3538948
  66.7 28.2 %collective-permute-start.11 = (bf16[2,384,768]{2,1,0:T(8,128)(2,1)S(1)}, bf16[2,384,768]{2,1,0:T(8,128)(2,1)S(1)}, u32[]{:S(2)}, u32[]{:S(2)}) collective-permute-start(bf16[2,384,768]{2,1,0:T(8,128)(2,1)S(1)} %collective-permute-done.9.refs_8_), channel_id=1, source_target_pairs={{0,32},{32,64},{64,96},{96,0},{1,33},{33,65},{65,97},{97,1},{2,34}... | collective-permute-start | bytes 3538952 | tf_op jit(solution)/shard_map/ppermute | solution.py:17
  68.1 29.6 %copy-start.8 = (bf16[2,384,768]{2,1,0:T(8,128)(2,1)}, bf16[2,384,768]{2,1,0:T(8,128)(2,1)S(1)}, u32[]{:S(2)}) copy-start(bf16[2,384,768]{2,1,0:T(8,128)(2,1)S(1)} %collective-permute-done.10.refs_9_) | copy-start | bytes 3538948
  68.1 28.3 %collective-permute-start.3 = (bf16[2,384,768]{2,1,0:T(8,128)(2,1)S(1)}, bf16[2,384,768]{2,1,0:T(8,128)(2,1)S(1)}, u32[]{:S(2)}, u32[]{:S(2)}) collective-permute-start(bf16[2,384,768]{2,1,0:T(8,128)(2,1)S(1)} %collective-permute-done.2.refs_2_), channel_id=1, source_target_pairs={{0,16},{16,0},{1,17},{17,1},{2,18},{18,2},{3,19},{19,3},{4,20},{20... | collective-permute-start | bytes 3538952 | tf_op jit(solution)/shard_map/ppermute | solution.py:17
  72.5 23.9 %copy-start.7 = (bf16[2,384,768]{2,1,0:T(8,128)(2,1)}, bf16[2,384,768]{2,1,0:T(8,128)(2,1)S(1)}, u32[]{:S(2)}) copy-start(bf16[2,384,768]{2,1,0:T(8,128)(2,1)S(1)} %collective-permute-done.5.refs_5_) | copy-start | bytes 3538948
  72.5 23.9 %collective-permute-start.8 = (bf16[2,384,768]{2,1,0:T(8,128)(2,1)S(1)}, bf16[2,384,768]{2,1,0:T(8,128)(2,1)S(1)}, u32[]{:S(2)}, u32[]{:S(2)}) collective-permute-start(bf16[2,384,768]{2,1,0:T(8,128)(2,1)S(1)} %pad_maximum_fusion.1.refs_6_), channel_id=1, source_target_pairs={{0,16},{16,0},{1,17},{17,1},{2,18},{18,2},{3,19},{19,3},{4,20},{20... | collective-permute-start | bytes 3538952 | tf_op jit(solution)/shard_map/ppermute | solution.py:17
  89.1 8.6 %copy-start.9 = (bf16[2,384,768]{2,1,0:T(8,128)(2,1)}, bf16[2,384,768]{2,1,0:T(8,128)(2,1)S(1)}, u32[]{:S(2)}) copy-start(bf16[2,384,768]{2,1,0:T(8,128)(2,1)S(1)} %collective-permute-done.15.refs_14_) | copy-start | bytes 3538948
  89.1 7.3 %collective-permute-start.16 = (bf16[2,384,768]{2,1,0:T(8,128)(2,1)S(1)}, bf16[2,384,768]{2,1,0:T(8,128)(2,1)S(1)}, u32[]{:S(2)}, u32[]{:S(2)}) collective-permute-start(bf16[2,384,768]{2,1,0:T(8,128)(2,1)S(1)} %collective-permute-done.15.refs_14_), channel_id=1, source_target_pairs={{0,16},{16,0},{1,17},{17,1},{2,18},{18,2},{3,19},{19,3},{4,20},{20... | collective-permute-start | bytes 3538952 | tf_op jit(solution)/shard_map/ppermute | solution.py:17
  93.5 4.2 %copy-start.10 = (bf16[2,384,768]{2,1,0:T(8,128)(2,1)}, bf16[2,384,768]{2,1,0:T(8,128)(2,1)S(1)}, u32[]{:S(2)}) copy-start(bf16[2,384,768]{2,1,0:T(8,128)(2,1)S(1)} %collective-permute-done.13.refs_12_) | copy-start | bytes 3538948
  93.5 4.2 %collective-permute-start.14 = (bf16[2,384,768]{2,1,0:T(8,128)(2,1)S(1)}, bf16[2,384,768]{2,1,0:T(8,128)(2,1)S(1)}, u32[]{:S(2)}, u32[]{:S(2)}) collective-permute-start(bf16[2,384,768]{2,1,0:T(8,128)(2,1)S(1)} %collective-permute-done.13.refs_12_), channel_id=1, source_target_pairs={{0,16},{16,0},{1,17},{17,1},{2,18},{18,2},{3,19},{19,3},{4,20},{20... | collective-permute-start | bytes 3538952 | tf_op jit(solution)/shard_map/ppermute | solution.py:17
  94.9 4.6 %copy-start.11 = (bf16[2,384,768]{2,1,0:T(8,128)(2,1)}, bf16[2,384,768]{2,1,0:T(8,128)(2,1)S(1)}, u32[]{:S(2)}) copy-start(bf16[2,384,768]{2,1,0:T(8,128)(2,1)S(1)} %collective-permute-done.11.refs_10_) | copy-start | bytes 3538948
  94.9 4.6 %collective-permute-start.12 = (bf16[2,384,768]{2,1,0:T(8,128)(2,1)S(1)}, bf16[2,384,768]{2,1,0:T(8,128)(2,1)}, u32[]{:S(2)}, u32[]{:S(2)}) collective-permute-start(bf16[2,384,768]{2,1,0:T(8,128)(2,1)S(1)} %collective-permute-done.11.refs_10_), channel_id=1, source_target_pairs={{0,16},{16,0},{1,17},{17,1},{2,18},{18,2},{3,19},{19,3},{4,20},{20... | collective-permute-start | bytes 3538952 | tf_op jit(solution)/shard_map/ppermute | solution.py:17
  96.4 1.3 %copy-start.12 = (bf16[2,384,768]{2,1,0:T(8,128)(2,1)}, bf16[2,384,768]{2,1,0:T(8,128)(2,1)S(1)}, u32[]{:S(2)}) copy-start(bf16[2,384,768]{2,1,0:T(8,128)(2,1)S(1)} %collective-permute-done.3.refs_3_) | copy-start | bytes 3538948
  96.4 3.1 %copy-start.13 = (bf16[2,384,768]{2,1,0:T(8,128)(2,1)}, bf16[2,384,768]{2,1,0:T(8,128)(2,1)S(1)}, u32[]{:S(2)}) copy-start(bf16[2,384,768]{2,1,0:T(8,128)(2,1)S(1)} %collective-permute-done.8.refs_7_) | copy-start | bytes 3538948
  96.4 1.4 %copy-start.14 = (bf16[2,384,768]{2,1,0:T(8,128)(2,1)}, bf16[2,384,768]{2,1,0:T(8,128)(2,1)S(1)}, u32[]{:S(2)}) copy-start(bf16[2,384,768]{2,1,0:T(8,128)(2,1)S(1)} %collective-permute-done.16.refs_15_) | copy-start | bytes 3538948
  97.8 1.1 copy-start.15
Sparse Core Ops, SparseCore 0:
  18.9 79.4 all-gather.1

commit v4 on v3

--- a/solution.py
+++ b/solution.py
@@ -25,7 +25,8 @@
 def multiply(origins, tokens_ref, *refs):
     y_hi, x, core = (lax.axis_index(name) for name in ROW)
     y_lo = lax.axis_index("y_lo")
-    weights, hidden, tokens, held, gate, up, token_sem, weight_sem = refs[:16], *refs[16:]
+    weights, refs = refs[:16], refs[16:]
+    hidden, tokens, held, gate, up, token_sem, weight_sem, write_sem = refs
     parts = len(weights) // 2
     depth = tokens_ref.shape[2]
 
@@ -60,16 +61,35 @@
             weight_copy(r, half).wait()
         if r + AHEAD < parts:
             start(r + AHEAD)
-        gate_part = jnp.dot(tokens[r], held[r, 0], preferred_element_type=jnp.float32)
-        up_part = jnp.dot(tokens[r], held[r, 1], preferred_element_type=jnp.float32)
-        if r == 0:
-            gate[...] = gate_part
-            up[...] = up_part
-        else:
-            gate[...] += gate_part
-            up[...] += up_part
-    value = gate[...]
-    hidden[...] = value / (1.0 + jnp.exp(-value)) * up[...]
+        if r < parts - 1:
+            gate_part = jnp.dot(tokens[r], held[r, 0], preferred_element_type=jnp.float32)
+            up_part = jnp.dot(tokens[r], held[r, 1], preferred_element_type=jnp.float32)
+            if r == 0:
+                gate[...] = gate_part
+                up[...] = up_part
+            else:
+                gate[...] += gate_part
+                up[...] += up_part
+    last, tile = parts - 1, 128
+    writes = []
+    for at in range(0, gate.shape[0], tile):
+        rows = slice(at, at + tile)
+        left = tokens[last, rows, :]
+        value = gate[rows, :] + jnp.dot(
+            left, held[last, 0], preferred_element_type=jnp.float32
+        )
+        times = up[rows, :] + jnp.dot(
+            left, held[last, 1], preferred_element_type=jnp.float32
+        )
+        gate[rows, :] = value / (1.0 + jnp.exp(-value)) * times
+        few = pl.ds(at, tile)
+        write = pltpu.make_async_copy(
+            gate.at[few, :], hidden.at[few, :], write_sem.at[at // tile]
+        )
+        write.start()
+        writes.append(write)
+    for write in writes:
+        write.wait()
 
 
 def per_device(tokens, gate_weight, up_weight):
@@ -77,8 +97,8 @@
     width = gate_weight.shape[1]
 
     own = jnp.stack([gate_weight, up_weight])
-    own, tokens = lax.optimization_barrier((own, tokens))
     other_tokens = shift(tokens, "y_lo", 2, 1)
+    own, other_tokens = lax.optimization_barrier((own, other_tokens))
     across = shift(own, "y_hi", 2, 1)
     own_1 = shift(own, "x", 4, 1)
     own_3 = shift(own, "x", 4, -1)
@@ -112,7 +132,7 @@
         functools.partial(multiply, origins),
         out_shape=jax.ShapeDtypeStruct((rows, width), jnp.float32),
         in_specs=[anywhere] * (1 + 2 * parts),
-        out_specs=pl.BlockSpec(memory_space=pltpu.VMEM),
+        out_specs=anywhere,
         scratch_shapes=[
             pltpu.VMEM((parts, rows, 2 * depth), tokens.dtype),
             pltpu.VMEM((parts, 2, 2 * depth, width), gate_weight.dtype),
@@ -120,6 +140,7 @@
             pltpu.VMEM((rows, width), jnp.float32),
             pltpu.SemaphoreType.DMA((parts, 2)),
             pltpu.SemaphoreType.DMA((parts, 2)),
+            pltpu.SemaphoreType.DMA((rows // 128,)),
         ],
         compiler_params=pltpu.CompilerParams(vmem_limit_bytes=58 * 1024 * 1024),
         cost_estimate=pl.CostEstimate(

time: 121 us -> 119 us (0.983)
  transfers between devices with their start and end apart: 18 -> 18, of which waited for: 7 -> 7; matrix products, arithmetic and copies ran while one was open for 0% -> 1% of each run, Pallas kernels for 0% -> 0%
where the time goes in v4:
time: 119 us
  waiting for transfers between devices  54.2 us (46%)
  starting transfers between devices  33.5 us (28%)
  Pallas kernels  13.8 us (12%)
  between operations  13.5 us (11%)
  other arithmetic  2.48 us (2%)
  local copies, waits for them, and re-layouts  1.35 us (1%)
    ppermute x17, waiting for transfers between devices, shift(): lax.ppermute(value, axis, [(i, (i + by) % size) for i in range(size)])  54.2 us
    ppermute x17, starting transfers between devices, shift(): lax.ppermute(value, axis, [(i, (i + by) % size) for i in range(size)])  33.5 us
    pallas_call x1, Pallas kernels, per_device(): pl.pallas_call(functools.partial(multiply, origins), out_shape=jax.ShapeD...  13.8 us
  transfers between devices with their start and end apart: 18, of which 7 were waited for; matrix products, arithmetic and copies ran while one was open for 1% of the time, Pallas kernels for 0%

profile of v4, /device:TPU:1, one launch (start us, length us, event | category | flops | bytes accessed | tf_op | source)
XLA Modules:
  0.0 118.8 jit_solution(14320315457175633469)
XLA Ops:
  6.5 0.0 all-gather.2.cloned.1.call-start
  6.5 2.1 %collective-permute-start = (bf16[512,384]{1,0:T(8,128)(2,1)}, bf16[512,384]{1,0:T(8,128)(2,1)S(1)}, u32[]{:S(2)}, u32[]{:S(2)}) collective-permute-start(bf16[512,384]{1,0:T(8,128)(2,1)} %param.3), channel_id=1, source_target_pairs={{0,8},{8,0},{1,9},{9,1},{2,10},{10,2},{3,11},{11,3},{4,12},{12,4},... | collective-permute-start | bytes 1179656 | tf_op jit(solution)/shard_map/ppermute | solution.py:17
  8.7 0.0 copy-start.2
  8.7 1.4 %pad_maximum_fusion.refs_0_ = bf16[2,384,768]{2,1,0:T(8,128)(2,1)S(1)} fusion(bf16[1,384,768]{2,1,0:T(8,128)(2,1)} %bitcast.10, bf16[1,384,768]{2,1,0:T(8,128)(2,1)} %bitcast.11), kind=kLoop, calls=%fused_computation | loop fusion | flops 589824 | bytes 2359296 | tf_op jit(solution)/shard_map/stack | solution.py:99
  10.1 0.0 copy-start
  10.1 6.5 %collective-permute-done = bf16[512,384]{1,0:T(8,128)(2,1)S(1)} collective-permute-done((bf16[512,384]{1,0:T(8,128)(2,1)}, bf16[512,384]{1,0:T(8,128)(2,1)S(1)}, u32[]{:S(2)}, u32[]{:S(2)}) %collective-permute-start) | collective-permute-done | bytes 393248 | tf_op jit(solution)/shard_map/ppermute | solution.py:17
  16.6 0.0 copy-done.2
  16.6 1.0 pad_maximum_fusion.2
  17.5 0.0 all-gather.2.cloned.1.call-update
  17.6 3.5 %collective-permute-start.4 = (bf16[2,384,768]{2,1,0:T(8,128)(2,1)S(1)}, bf16[2,384,768]{2,1,0:T(8,128)(2,1)S(1)}, u32[]{:S(2)}, u32[]{:S(2)}) collective-permute-start(bf16[2,384,768]{2,1,0:T(8,128)(2,1)S(1)} %pad_maximum_fusion.refs_0_), channel_id=1, source_target_pairs={{0,96},{32,0},{64,32},{96,64},{1,97},{33,1},{65,33},{97,65},{2,98}... | collective-permute-start | bytes 3538952 | tf_op jit(solution)/shard_map/ppermute | solution.py:17
  21.1 0.0 collective-permute-start.2
  21.1 2.9 %collective-permute-start.9 = (bf16[2,384,768]{2,1,0:T(8,128)(2,1)S(1)}, bf16[2,384,768]{2,1,0:T(8,128)(2,1)S(1)}, u32[]{:S(2)}, u32[]{:S(2)}) collective-permute-start(bf16[2,384,768]{2,1,0:T(8,128)(2,1)S(1)} %pad_maximum_fusion.refs_0_), channel_id=1, source_target_pairs={{0,128},{128,0},{1,129},{129,1},{2,130},{130,2},{3,131},{131,3},{4... | collective-permute-start | bytes 3538952 | tf_op jit(solution)/shard_map/ppermute | solution.py:17
  24.0 0.0 copy-done
  24.0 2.1 %collective-permute-start.1 = (bf16[2,384,768]{2,1,0:T(8,128)(2,1)S(1)}, bf16[2,384,768]{2,1,0:T(8,128)(2,1)S(1)}, u32[]{:S(2)}, u32[]{:S(2)}) collective-permute-start(bf16[2,384,768]{2,1,0:T(8,128)(2,1)S(1)} %pad_maximum_fusion.refs_0_), channel_id=1, source_target_pairs={{0,16},{16,0},{1,17},{17,1},{2,18},{18,2},{3,19},{19,3},{4,20},{20... | collective-permute-start | bytes 3538952 | tf_op jit(solution)/shard_map/ppermute | solution.py:17
  26.1 18.7 %collective-permute-done.4.refs_4_ = bf16[2,384,768]{2,1,0:T(8,128)(2,1)S(1)} collective-permute-done((bf16[2,384,768]{2,1,0:T(8,128)(2,1)S(1)}, bf16[2,384,768]{2,1,0:T(8,128)(2,1)S(1)}, u32[]{:S(2)}, u32[]{:S(2)}) %collective-permute-start.4) | collective-permute-done | bytes 1179680 | tf_op jit(solution)/shard_map/ppermute | solution.py:17
  44.8 0.0 copy-start.3
  44.9 3.6 %collective-permute-start.7 = (bf16[384,768]{1,0:T(8,128)(2,1)S(1)}, bf16[384,768]{1,0:T(8,128)(2,1)S(1)}, u32[]{:S(2)}, u32[]{:S(2)}) collective-permute-start(bf16[384,768]{1,0:T(8,128)(2,1)S(1)} %slice_bitcast_fusion), channel_id=1, source_target_pairs={{0,96},{32,0},{64,32},{96,64},{1,97},{33,1},{65,33},{97,65},{2,98}... | collective-permute-start | bytes 1769480 | tf_op jit(solution)/shard_map/ppermute | solution.py:17
  48.5 0.0 collective-permute-done.2.refs_2_
  48.5 0.0 copy-start.4
  48.5 0.1 collective-permute-start.6
  48.6 2.7 %collective-permute-start.5 = (bf16[2,384,768]{2,1,0:T(8,128)(2,1)S(1)}, bf16[2,384,768]{2,1,0:T(8,128)(2,1)S(1)}, u32[]{:S(2)}, u32[]{:S(2)}) collective-permute-start(bf16[2,384,768]{2,1,0:T(8,128)(2,1)S(1)} %collective-permute-done.4.refs_4_), channel_id=1, source_target_pairs={{0,16},{16,0},{1,17},{17,1},{2,18},{18,2},{3,19},{19,3},{4,20},{20... | collective-permute-start | bytes 3538952 | tf_op jit(solution)/shard_map/ppermute | solution.py:17
  51.3 0.0 collective-permute-done.9.refs_8_
  51.3 0.0 copy-start.5
  51.3 0.1 collective-permute-start.10
  51.5 7.3 %collective-permute-done.7 = bf16[384,768]{1,0:T(8,128)(2,1)S(1)} collective-permute-done((bf16[384,768]{1,0:T(8,128)(2,1)S(1)}, bf16[384,768]{1,0:T(8,128)(2,1)S(1)}, u32[]{:S(2)}, u32[]{:S(2)}) %collective-permute-start.7) | collective-permute-done | bytes 589856 | tf_op jit(solution)/shard_map/ppermute | solution.py:17
  58.7 3.4 %collective-permute-done.6 = bf16[384,768]{1,0:T(8,128)(2,1)S(1)} collective-permute-done((bf16[384,768]{1,0:T(8,128)(2,1)S(1)}, bf16[384,768]{1,0:T(8,128)(2,1)S(1)}, u32[]{:S(2)}, u32[]{:S(2)}) %collective-permute-start.6) | collective-permute-done | bytes 589856 | tf_op jit(solution)/shard_map/ppermute | solution.py:17
  62.1 0.0 copy-done.3
  62.1 0.1 pad_maximum_fusion.1.refs_6_
  62.2 0.0 copy-start.1
  62.2 3.0 %collective-permute-start.15 = (bf16[2,384,768]{2,1,0:T(8,128)(2,1)S(1)}, bf16[2,384,768]{2,1,0:T(8,128)(2,1)S(1)}, u32[]{:S(2)}, u32[]{:S(2)}) collective-permute-start(bf16[2,384,768]{2,1,0:T(8,128)(2,1)S(1)} %pad_maximum_fusion.1.refs_6_), channel_id=1, source_target_pairs={{0,128},{128,0},{1,129},{129,1},{2,130},{130,2},{3,131},{131,3},{4... | collective-permute-start | bytes 3538952 | tf_op jit(solution)/shard_map/ppermute | solution.py:17
  65.2 0.2 collective-permute-start.13
  65.4 0.0 collective-permute-done.1.refs_1_
  65.4 0.0 copy-done.5
  65.4 1.4 %collective-permute-start.11 = (bf16[2,384,768]{2,1,0:T(8,128)(2,1)S(1)}, bf16[2,384,768]{2,1,0:T(8,128)(2,1)S(1)}, u32[]{:S(2)}, u32[]{:S(2)}) collective-permute-start(bf16[2,384,768]{2,1,0:T(8,128)(2,1)S(1)} %collective-permute-done.9.refs_8_), channel_id=1, source_target_pairs={{0,32},{32,64},{64,96},{96,0},{1,33},{33,65},{65,97},{97,1},{2,34}... | collective-permute-start | bytes 3538952 | tf_op jit(solution)/shard_map/ppermute | solution.py:17
  66.8 0.0 collective-permute-done.10.refs_9_
  66.8 0.0 copy-done.4
  66.8 4.4 %collective-permute-start.3 = (bf16[2,384,768]{2,1,0:T(8,128)(2,1)S(1)}, bf16[2,384,768]{2,1,0:T(8,128)(2,1)S(1)}, u32[]{:S(2)}, u32[]{:S(2)}) collective-permute-start(bf16[2,384,768]{2,1,0:T(8,128)(2,1)S(1)} %collective-permute-done.2.refs_2_), channel_id=1, source_target_pairs={{0,16},{16,0},{1,17},{17,1},{2,18},{18,2},{3,19},{19,3},{4,20},{20... | collective-permute-start | bytes 3538952 | tf_op jit(solution)/shard_map/ppermute | solution.py:17
  71.2 0.0 collective-permute-done.5.refs_5_
  71.2 0.1 collective-permute-start.8
  71.3 16.5 %collective-permute-done.15.refs_14_ = bf16[2,384,768]{2,1,0:T(8,128)(2,1)S(1)} collective-permute-done((bf16[2,384,768]{2,1,0:T(8,128)(2,1)S(1)}, bf16[2,384,768]{2,1,0:T(8,128)(2,1)S(1)}, u32[]{:S(2)}, u32[]{:S(2)}) %collective-permute-start.15) | collective-permute-done | bytes 1179680 | tf_op jit(solution)/shard_map/ppermute | solution.py:17
  87.8 4.4 %collective-permute-start.16 = (bf16[2,384,768]{2,1,0:T(8,128)(2,1)S(1)}, bf16[2,384,768]{2,1,0:T(8,128)(2,1)S(1)}, u32[]{:S(2)}, u32[]{:S(2)}) collective-permute-start(bf16[2,384,768]{2,1,0:T(8,128)(2,1)S(1)} %collective-permute-done.15.refs_14_), channel_id=1, source_target_pairs={{0,16},{16,0},{1,17},{17,1},{2,18},{18,2},{3,19},{19,3},{4,20},{20... | collective-permute-start | bytes 3538952 | tf_op jit(solution)/shard_map/ppermute | solution.py:17
  92.2 0.0 collective-permute-done.13.refs_12_
  92.2 1.4 %collective-permute-start.14 = (bf16[2,384,768]{2,1,0:T(8,128)(2,1)S(1)}, bf16[2,384,768]{2,1,0:T(8,128)(2,1)S(1)}, u32[]{:S(2)}, u32[]{:S(2)}) collective-permute-start(bf16[2,384,768]{2,1,0:T(8,128)(2,1)S(1)} %collective-permute-done.13.refs_12_), channel_id=1, source_target_pairs={{0,16},{16,0},{1,17},{17,1},{2,18},{18,2},{3,19},{19,3},{4,20},{20... | collective-permute-start | bytes 3538952 | tf_op jit(solution)/shard_map/ppermute | solution.py:17
  93.6 0.0 collective-permute-done.11.refs_10_
  93.6 1.4 %collective-permute-start.12 = (bf16[2,384,768]{2,1,0:T(8,128)(2,1)S(1)}, bf16[2,384,768]{2,1,0:T(8,128)(2,1)}, u32[]{:S(2)}, u32[]{:S(2)}) collective-permute-start(bf16[2,384,768]{2,1,0:T(8,128)(2,1)S(1)} %collective-permute-done.11.refs_10_), channel_id=1, source_target_pairs={{0,16},{16,0},{1,17},{17,1},{2,18},{18,2},{3,19},{19,3},{4,20},{20... | collective-permute-start | bytes 3538952 | tf_op jit(solution)/shard_map/ppermute | solution.py:17
  95.1 0.0 collective-permute-done.3.refs_3_
  95.1 0.0 collective-permute-done.8.refs_7_
  95.1 0.0 copy-done.6
  95.1 0.0 copy-start.13
  95.1 0.0 collective-permute-done.16.refs_15_
  95.1 0.0 copy-done.7
  95.1 0.0 copy-start.14
  95.1 1.2 %collective-permute-done.14.refs_13_ = bf16[2,384,768]{2,1,0:T(8,128)(2,1)S(1)} collective-permute-done((bf16[2,384,768]{2,1,0:T(8,128)(2,1)S(1)}, bf16[2,384,768]{2,1,0:T(8,128)(2,1)S(1)}, u32[]{:S(2)}, u32[]{:S(2)}) %collective-permute-start.14) | collective-permute-done | bytes 1179680 | tf_op jit(solution)/shard_map/ppermute | solution.py:17
  96.4 0.0 copy-done.8
  96.4 0.0 copy-done.9
  96.4 0.0 copy-done.10
  96.4 0.0 copy-done.12
  96.4 0.2 copy-done.14
  96.5 1.1 copy-done.15
  97.6 0.6 collective-permute-done.12.refs_11_
  98.2 0.0 copy-done.1
  98.2 0.0 copy-done.11
  98.2 0.0 copy-done.13
  98.2 13.8 %shard_map.37 = f32[512,768]{1,0:T(8,128)} custom-call(bf16[16,512,384]{2,1,0:T(8,128)(2,1)} %all-gather.2.cloned.1.call-done.tokens_ref, bf16[2,384,768]{2,1,0:T(8,128)(2,1)} %copy-done, bf16[2,384,768]{2,1,0:T(8,128)(2,1)} %copy-done.6, bf16[2,384,768]{2,1,0:T(8,128)(2,1)} %copy-done.4, bf16[2,384,768]{2,1,0:T(8,128)(2,1)} %copy-done.12, ...), custom_call_target="tpu_custom_call" | custom-call | flops 9663676416 | bytes 26738688 | tf_op jit(solution)/shard_map/pallas_call | solution.py:131
  (11 shorter events, 0.1 us)
Async XLA Ops:
  6.5 91.6 %all-gather.2.cloned.1.call-start = ((), (), s32[]{:S(2)}) async-start(), calls=%async_computation | async-start | bytes 7077888 | tf_op jit(solution)/shard_map/all_gather | solution.py:109
  6.5 10.0 %collective-permute-start = (bf16[512,384]{1,0:T(8,128)(2,1)}, bf16[512,384]{1,0:T(8,128)(2,1)S(1)}, u32[]{:S(2)}, u32[]{:S(2)}) collective-permute-start(bf16[512,384]{1,0:T(8,128)(2,1)} %param.3), channel_id=1, source_target_pairs={{0,8},{8,0},{1,9},{9,1},{2,10},{10,2},{3,11},{11,3},{4,12},{12,4},... | collective-permute-start | bytes 1179656 | tf_op jit(solution)/shard_map/ppermute | solution.py:17
  8.7 7.9 %copy-start.2 = (bf16[512,384]{1,0:T(8,128)(2,1)S(1)}, bf16[512,384]{1,0:T(8,128)(2,1)}, u32[]{:S(2)}) copy-start(bf16[512,384]{1,0:T(8,128)(2,1)} %param.3) | copy-start | bytes 1179652
  10.1 14.0 %copy-start = (bf16[2,384,768]{2,1,0:T(8,128)(2,1)}, bf16[2,384,768]{2,1,0:T(8,128)(2,1)S(1)}, u32[]{:S(2)}) copy-start(bf16[2,384,768]{2,1,0:T(8,128)(2,1)S(1)} %pad_maximum_fusion.refs_0_) | copy-start | bytes 3538948
  17.6 27.3 %collective-permute-start.4 = (bf16[2,384,768]{2,1,0:T(8,128)(2,1)S(1)}, bf16[2,384,768]{2,1,0:T(8,128)(2,1)S(1)}, u32[]{:S(2)}, u32[]{:S(2)}) collective-permute-start(bf16[2,384,768]{2,1,0:T(8,128)(2,1)S(1)} %pad_maximum_fusion.refs_0_), channel_id=1, source_target_pairs={{0,96},{32,0},{64,32},{96,64},{1,97},{33,1},{65,33},{97,65},{2,98}... | collective-permute-start | bytes 3538952 | tf_op jit(solution)/shard_map/ppermute | solution.py:17
  21.1 27.4 %collective-permute-start.2 = (bf16[2,384,768]{2,1,0:T(8,128)(2,1)S(1)}, bf16[2,384,768]{2,1,0:T(8,128)(2,1)S(1)}, u32[]{:S(2)}, u32[]{:S(2)}) collective-permute-start(bf16[2,384,768]{2,1,0:T(8,128)(2,1)S(1)} %pad_maximum_fusion.refs_0_), channel_id=1, source_target_pairs={{0,32},{32,64},{64,96},{96,0},{1,33},{33,65},{65,97},{97,1},{2,34}... | collective-permute-start | bytes 3538952 | tf_op jit(solution)/shard_map/ppermute | solution.py:17
  21.1 30.2 %collective-permute-start.9 = (bf16[2,384,768]{2,1,0:T(8,128)(2,1)S(1)}, bf16[2,384,768]{2,1,0:T(8,128)(2,1)S(1)}, u32[]{:S(2)}, u32[]{:S(2)}) collective-permute-start(bf16[2,384,768]{2,1,0:T(8,128)(2,1)S(1)} %pad_maximum_fusion.refs_0_), channel_id=1, source_target_pairs={{0,128},{128,0},{1,129},{129,1},{2,130},{130,2},{3,131},{131,3},{4... | collective-permute-start | bytes 3538952 | tf_op jit(solution)/shard_map/ppermute | solution.py:17
  24.0 41.3 %collective-permute-start.1 = (bf16[2,384,768]{2,1,0:T(8,128)(2,1)S(1)}, bf16[2,384,768]{2,1,0:T(8,128)(2,1)S(1)}, u32[]{:S(2)}, u32[]{:S(2)}) collective-permute-start(bf16[2,384,768]{2,1,0:T(8,128)(2,1)S(1)} %pad_maximum_fusion.refs_0_), channel_id=1, source_target_pairs={{0,16},{16,0},{1,17},{17,1},{2,18},{18,2},{3,19},{19,3},{4,20},{20... | collective-permute-start | bytes 3538952 | tf_op jit(solution)/shard_map/ppermute | solution.py:17
  44.8 17.3 %copy-start.3 = (bf16[2,384,768]{2,1,0:T(8,128)(2,1)}, bf16[2,384,768]{2,1,0:T(8,128)(2,1)S(1)}, u32[]{:S(2)}) copy-start(bf16[2,384,768]{2,1,0:T(8,128)(2,1)S(1)} %collective-permute-done.4.refs_4_) | copy-start | bytes 3538948
  44.9 13.9 %collective-permute-start.7 = (bf16[384,768]{1,0:T(8,128)(2,1)S(1)}, bf16[384,768]{1,0:T(8,128)(2,1)S(1)}, u32[]{:S(2)}, u32[]{:S(2)}) collective-permute-start(bf16[384,768]{1,0:T(8,128)(2,1)S(1)} %slice_bitcast_fusion), channel_id=1, source_target_pairs={{0,96},{32,0},{64,32},{96,64},{1,97},{33,1},{65,33},{97,65},{2,98}... | collective-permute-start | bytes 1769480 | tf_op jit(solution)/shard_map/ppermute | solution.py:17
  48.5 18.3 %copy-start.4 = (bf16[2,384,768]{2,1,0:T(8,128)(2,1)}, bf16[2,384,768]{2,1,0:T(8,128)(2,1)S(1)}, u32[]{:S(2)}) copy-start(bf16[2,384,768]{2,1,0:T(8,128)(2,1)S(1)} %collective-permute-done.2.refs_2_) | copy-start | bytes 3538948
  48.5 13.6 %collective-permute-start.6 = (bf16[384,768]{1,0:T(8,128)(2,1)S(1)}, bf16[384,768]{1,0:T(8,128)(2,1)S(1)}, u32[]{:S(2)}, u32[]{:S(2)}) collective-permute-start(bf16[384,768]{1,0:T(8,128)(2,1)S(1)} %slice_bitcast_fusion.1), channel_id=1, source_target_pairs={{0,32},{32,64},{64,96},{96,0},{1,33},{33,65},{65,97},{97,1},{2,34}... | collective-permute-start | bytes 1769480 | tf_op jit(solution)/shard_map/ppermute | solution.py:17
  48.6 22.5 %collective-permute-start.5 = (bf16[2,384,768]{2,1,0:T(8,128)(2,1)S(1)}, bf16[2,384,768]{2,1,0:T(8,128)(2,1)S(1)}, u32[]{:S(2)}, u32[]{:S(2)}) collective-permute-start(bf16[2,384,768]{2,1,0:T(8,128)(2,1)S(1)} %collective-permute-done.4.refs_4_), channel_id=1, source_target_pairs={{0,16},{16,0},{1,17},{17,1},{2,18},{18,2},{3,19},{19,3},{4,20},{20... | collective-permute-start | bytes 3538952 | tf_op jit(solution)/shard_map/ppermute | solution.py:17
  51.3 14.0 %copy-start.5 = (bf16[2,384,768]{2,1,0:T(8,128)(2,1)}, bf16[2,384,768]{2,1,0:T(8,128)(2,1)S(1)}, u32[]{:S(2)}) copy-start(bf16[2,384,768]{2,1,0:T(8,128)(2,1)S(1)} %collective-permute-done.9.refs_8_) | copy-start | bytes 3538948
  51.3 15.4 %collective-permute-start.10 = (bf16[2,384,768]{2,1,0:T(8,128)(2,1)S(1)}, bf16[2,384,768]{2,1,0:T(8,128)(2,1)S(1)}, u32[]{:S(2)}, u32[]{:S(2)}) collective-permute-start(bf16[2,384,768]{2,1,0:T(8,128)(2,1)S(1)} %collective-permute-done.9.refs_8_), channel_id=1, source_target_pairs={{0,16},{16,0},{1,17},{17,1},{2,18},{18,2},{3,19},{19,3},{4,20},{20... | collective-permute-start | bytes 3538952 | tf_op jit(solution)/shard_map/ppermute | solution.py:17
  62.2 36.0 %copy-start.1 = (bf16[2,384,768]{2,1,0:T(8,128)(2,1)}, bf16[2,384,768]{2,1,0:T(8,128)(2,1)S(1)}, u32[]{:S(2)}) copy-start(bf16[2,384,768]{2,1,0:T(8,128)(2,1)S(1)} %pad_maximum_fusion.1.refs_6_) | copy-start | bytes 3538948
  62.2 25.6 %collective-permute-start.15 = (bf16[2,384,768]{2,1,0:T(8,128)(2,1)S(1)}, bf16[2,384,768]{2,1,0:T(8,128)(2,1)S(1)}, u32[]{:S(2)}, u32[]{:S(2)}) collective-permute-start(bf16[2,384,768]{2,1,0:T(8,128)(2,1)S(1)} %pad_maximum_fusion.1.refs_6_), channel_id=1, source_target_pairs={{0,128},{128,0},{1,129},{129,1},{2,130},{130,2},{3,131},{131,3},{4... | collective-permute-start | bytes 3538952 | tf_op jit(solution)/shard_map/ppermute | solution.py:17
  65.2 27.0 %collective-permute-start.13 = (bf16[2,384,768]{2,1,0:T(8,128)(2,1)S(1)}, bf16[2,384,768]{2,1,0:T(8,128)(2,1)S(1)}, u32[]{:S(2)}, u32[]{:S(2)}) collective-permute-start(bf16[2,384,768]{2,1,0:T(8,128)(2,1)S(1)} %collective-permute-done.9.refs_8_), channel_id=1, source_target_pairs={{0,96},{32,0},{64,32},{96,64},{1,97},{33,1},{65,33},{97,65},{2,98}... | collective-permute-start | bytes 3538952 | tf_op jit(solution)/shard_map/ppermute | solution.py:17
  65.4 29.7 %copy-start.6 = (bf16[2,384,768]{2,1,0:T(8,128)(2,1)}, bf16[2,384,768]{2,1,0:T(8,128)(2,1)S(1)}, u32[]{:S(2)}) copy-start(bf16[2,384,768]{2,1,0:T(8,128)(2,1)S(1)} %collective-permute-done.1.refs_1_) | copy-start | bytes 3538948
  65.4 28.2 %collective-permute-start.11 = (bf16[2,384,768]{2,1,0:T(8,128)(2,1)S(1)}, bf16[2,384,768]{2,1,0:T(8,128)(2,1)S(1)}, u32[]{:S(2)}, u32[]{:S(2)}) collective-permute-start(bf16[2,384,768]{2,1,0:T(8,128)(2,1)S(1)} %collective-permute-done.9.refs_8_), channel_id=1, source_target_pairs={{0,32},{32,64},{64,96},{96,0},{1,33},{33,65},{65,97},{97,1},{2,34}... | collective-permute-start | bytes 3538952 | tf_op jit(solution)/shard_map/ppermute | solution.py:17
  66.8 29.6 %copy-start.8 = (bf16[2,384,768]{2,1,0:T(8,128)(2,1)}, bf16[2,384,768]{2,1,0:T(8,128)(2,1)S(1)}, u32[]{:S(2)}) copy-start(bf16[2,384,768]{2,1,0:T(8,128)(2,1)S(1)} %collective-permute-done.10.refs_9_) | copy-start | bytes 3538948
  66.8 28.3 %collective-permute-start.3 = (bf16[2,384,768]{2,1,0:T(8,128)(2,1)S(1)}, bf16[2,384,768]{2,1,0:T(8,128)(2,1)S(1)}, u32[]{:S(2)}, u32[]{:S(2)}) collective-permute-start(bf16[2,384,768]{2,1,0:T(8,128)(2,1)S(1)} %collective-permute-done.2.refs_2_), channel_id=1, source_target_pairs={{0,16},{16,0},{1,17},{17,1},{2,18},{18,2},{3,19},{19,3},{4,20},{20... | collective-permute-start | bytes 3538952 | tf_op jit(solution)/shard_map/ppermute | solution.py:17
  71.2 23.9 %copy-start.7 = (bf16[2,384,768]{2,1,0:T(8,128)(2,1)}, bf16[2,384,768]{2,1,0:T(8,128)(2,1)S(1)}, u32[]{:S(2)}) copy-start(bf16[2,384,768]{2,1,0:T(8,128)(2,1)S(1)} %collective-permute-done.5.refs_5_) | copy-start | bytes 3538948
  71.2 23.9 %collective-permute-start.8 = (bf16[2,384,768]{2,1,0:T(8,128)(2,1)S(1)}, bf16[2,384,768]{2,1,0:T(8,128)(2,1)S(1)}, u32[]{:S(2)}, u32[]{:S(2)}) collective-permute-start(bf16[2,384,768]{2,1,0:T(8,128)(2,1)S(1)} %pad_maximum_fusion.1.refs_6_), channel_id=1, source_target_pairs={{0,16},{16,0},{1,17},{17,1},{2,18},{18,2},{3,19},{19,3},{4,20},{20... | collective-permute-start | bytes 3538952 | tf_op jit(solution)/shard_map/ppermute | solution.py:17
  87.8 8.6 %copy-start.9 = (bf16[2,384,768]{2,1,0:T(8,128)(2,1)}, bf16[2,384,768]{2,1,0:T(8,128)(2,1)S(1)}, u32[]{:S(2)}) copy-start(bf16[2,384,768]{2,1,0:T(8,128)(2,1)S(1)} %collective-permute-done.15.refs_14_) | copy-start | bytes 3538948
  87.8 7.3 %collective-permute-start.16 = (bf16[2,384,768]{2,1,0:T(8,128)(2,1)S(1)}, bf16[2,384,768]{2,1,0:T(8,128)(2,1)S(1)}, u32[]{:S(2)}, u32[]{:S(2)}) collective-permute-start(bf16[2,384,768]{2,1,0:T(8,128)(2,1)S(1)} %collective-permute-done.15.refs_14_), channel_id=1, source_target_pairs={{0,16},{16,0},{1,17},{17,1},{2,18},{18,2},{3,19},{19,3},{4,20},{20... | collective-permute-start | bytes 3538952 | tf_op jit(solution)/shard_map/ppermute | solution.py:17
  92.2 4.2 %copy-start.10 = (bf16[2,384,768]{2,1,0:T(8,128)(2,1)}, bf16[2,384,768]{2,1,0:T(8,128)(2,1)S(1)}, u32[]{:S(2)}) copy-start(bf16[2,384,768]{2,1,0:T(8,128)(2,1)S(1)} %collective-permute-done.13.refs_12_) | copy-start | bytes 3538948
  92.2 4.2 %collective-permute-start.14 = (bf16[2,384,768]{2,1,0:T(8,128)(2,1)S(1)}, bf16[2,384,768]{2,1,0:T(8,128)(2,1)S(1)}, u32[]{:S(2)}, u32[]{:S(2)}) collective-permute-start(bf16[2,384,768]{2,1,0:T(8,128)(2,1)S(1)} %collective-permute-done.13.refs_12_), channel_id=1, source_target_pairs={{0,16},{16,0},{1,17},{17,1},{2,18},{18,2},{3,19},{19,3},{4,20},{20... | collective-permute-start | bytes 3538952 | tf_op jit(solution)/shard_map/ppermute | solution.py:17
  93.6 4.6 %copy-start.11 = (bf16[2,384,768]{2,1,0:T(8,128)(2,1)}, bf16[2,384,768]{2,1,0:T(8,128)(2,1)S(1)}, u32[]{:S(2)}) copy-start(bf16[2,384,768]{2,1,0:T(8,128)(2,1)S(1)} %collective-permute-done.11.refs_10_) | copy-start | bytes 3538948
  93.6 4.6 %collective-permute-start.12 = (bf16[2,384,768]{2,1,0:T(8,128)(2,1)S(1)}, bf16[2,384,768]{2,1,0:T(8,128)(2,1)}, u32[]{:S(2)}, u32[]{:S(2)}) collective-permute-start(bf16[2,384,768]{2,1,0:T(8,128)(2,1)S(1)} %collective-permute-done.11.refs_10_), channel_id=1, source_target_pairs={{0,16},{16,0},{1,17},{17,1},{2,18},{18,2},{3,19},{19,3},{4,20},{20... | collective-permute-start | bytes 3538952 | tf_op jit(solution)/shard_map/ppermute | solution.py:17
  95.1 1.3 %copy-start.12 = (bf16[2,384,768]{2,1,0:T(8,128)(2,1)}, bf16[2,384,768]{2,1,0:T(8,128)(2,1)S(1)}, u32[]{:S(2)}) copy-start(bf16[2,384,768]{2,1,0:T(8,128)(2,1)S(1)} %collective-permute-done.3.refs_3_) | copy-start | bytes 3538948
  95.1 3.1 %copy-start.13 = (bf16[2,384,768]{2,1,0:T(8,128)(2,1)}, bf16[2,384,768]{2,1,0:T(8,128)(2,1)S(1)}, u32[]{:S(2)}) copy-start(bf16[2,384,768]{2,1,0:T(8,128)(2,1)S(1)} %collective-permute-done.8.refs_7_) | copy-start | bytes 3538948
  95.1 1.4 %copy-start.14 = (bf16[2,384,768]{2,1,0:T(8,128)(2,1)}, bf16[2,384,768]{2,1,0:T(8,128)(2,1)S(1)}, u32[]{:S(2)}) copy-start(bf16[2,384,768]{2,1,0:T(8,128)(2,1)S(1)} %collective-permute-done.16.refs_15_) | copy-start | bytes 3538948
  96.5 1.1 copy-start.15
Sparse Core Ops, SparseCore 0:
  17.7 79.2 all-gather.1

commit v5 on v4

--- a/solution.py
+++ b/solution.py
@@ -98,16 +98,18 @@
 
     own = jnp.stack([gate_weight, up_weight])
     other_tokens = shift(tokens, "y_lo", 2, 1)
-    own, other_tokens = lax.optimization_barrier((own, other_tokens))
+    room = jnp.zeros((2, rows, depth), tokens.dtype)
+    room = lax.dynamic_update_slice(room, tokens[None], (0, 0, 0))
+    own, room, other_tokens = lax.optimization_barrier((own, room, other_tokens))
     across = shift(own, "y_hi", 2, 1)
     own_1 = shift(own, "x", 4, 1)
     own_3 = shift(own, "x", 4, -1)
     own_2g = shift(own_1[0], "x", 4, 1)
     own_2u = shift(own_3[1], "x", 4, -1)
     own_2 = jnp.stack([own_2g, own_2u])
-    pair = jnp.stack([tokens, other_tokens])
+    pair = lax.dynamic_update_slice(room, other_tokens[None], (1, 0, 0))
     gathered = lax.all_gather(pair, "z", axis=0, tiled=True)
-    (across_late,) = after([own_2g, own_2u], across)
+    (across_late,) = after([own_2u], across)
     across_1 = shift(across_late, "x", 4, 1)
     across_3 = shift(across_late, "x", 4, -1)
     across_2 = shift(own_2, "y_hi", 2, 1)

time: 119 us -> 118 us (level)
  waiting for transfers between devices: 54.2 us -> 51.1 us
  other arithmetic: 2.48 us -> 0.22 us
  starting transfers between devices: 33.5 us -> 35.7 us
  local copies, waits for them, and re-layouts: 1.35 us -> 3.18 us
    ppermute x17, waiting for transfers between devices: 54.2 us -> 50.2 us  [shift(): lax.ppermute(value, axis, [(i, (i + by) % size) for i in range(size)])]
    ppermute x17, starting transfers between devices: 33.5 us -> 35.7 us  [shift(): lax.ppermute(value, axis, [(i, (i + by) % size) for i in range(size)])]
    another operation x1, other arithmetic: 1.4 us -> 0.11 us  [per_device(): own = jnp.stack([gate_weight, up_weight])]
where the time goes in v5:
time: 118 us
  waiting for transfers between devices  51.1 us (43%)
  starting transfers between devices  35.7 us (30%)
  Pallas kernels  13.8 us (12%)
  between operations  13.6 us (12%)
  local copies, waits for them, and re-layouts  3.18 us (3%)
    ppermute x17, waiting for transfers between devices, shift(): lax.ppermute(value, axis, [(i, (i + by) % size) for i in range(size)])  50.2 us
    ppermute x17, starting transfers between devices, shift(): lax.ppermute(value, axis, [(i, (i + by) % size) for i in range(size)])  35.7 us
    pallas_call x1, Pallas kernels, per_device(): pl.pallas_call(functools.partial(multiply, origins), out_shape=jax.ShapeD...  13.8 us
  transfers between devices with their start and end apart: 18, of which 7 were waited for; matrix products, arithmetic and copies ran while one was open for 1% of the time, Pallas kernels for 0%

profile of v5, /device:TPU:1, one launch (start us, length us, event | category | flops | bytes accessed | tf_op | source)
XLA Modules:
  0.0 117.6 jit_solution(2285082596090095732)
XLA Ops:
  6.5 0.0 all-gather.2.cloned.1.call-start
  6.5 2.1 %collective-permute-start = (bf16[512,384]{1,0:T(8,128)(2,1)}, bf16[512,384]{1,0:T(8,128)(2,1)S(1)}, u32[]{:S(2)}, u32[]{:S(2)}) collective-permute-start(bf16[512,384]{1,0:T(8,128)(2,1)} %param.3), channel_id=1, source_target_pairs={{0,8},{8,0},{1,9},{9,1},{2,10},{10,2},{3,11},{11,3},{4,12},{12,4},... | collective-permute-start | bytes 1179656 | tf_op jit(solution)/shard_map/ppermute | solution.py:17
  8.7 1.1 dynamic_update_slice.6
  9.8 0.0 copy-done.3
  9.8 0.0 copy-done.4
  9.8 0.1 pad_maximum_fusion.refs_0_
  9.9 0.0 copy-start.1
  9.9 6.7 %collective-permute-done = bf16[512,384]{1,0:T(8,128)(2,1)S(1)} collective-permute-done((bf16[512,384]{1,0:T(8,128)(2,1)}, bf16[512,384]{1,0:T(8,128)(2,1)S(1)}, u32[]{:S(2)}, u32[]{:S(2)}) %collective-permute-start) | collective-permute-done | bytes 393248 | tf_op jit(solution)/shard_map/ppermute | solution.py:17
  16.6 0.1 bitcast_dynamic-update-slice_fusion
  16.6 0.0 copy-start
  16.7 0.9 copy-done
  17.5 0.0 all-gather.2.cloned.1.call-update
  17.6 3.5 %collective-permute-start.4 = (bf16[2,384,768]{2,1,0:T(8,128)(2,1)S(1)}, bf16[2,384,768]{2,1,0:T(8,128)(2,1)S(1)}, u32[]{:S(2)}, u32[]{:S(2)}) collective-permute-start(bf16[2,384,768]{2,1,0:T(8,128)(2,1)S(1)} %pad_maximum_fusion.refs_0_), channel_id=1, source_target_pairs={{0,96},{32,0},{64,32},{96,64},{1,97},{33,1},{65,33},{97,65},{2,98}... | collective-permute-start | bytes 3538952 | tf_op jit(solution)/shard_map/ppermute | solution.py:17
  21.1 0.0 collective-permute-start.2
  21.1 2.9 %collective-permute-start.9 = (bf16[2,384,768]{2,1,0:T(8,128)(2,1)S(1)}, bf16[2,384,768]{2,1,0:T(8,128)(2,1)S(1)}, u32[]{:S(2)}, u32[]{:S(2)}) collective-permute-start(bf16[2,384,768]{2,1,0:T(8,128)(2,1)S(1)} %pad_maximum_fusion.refs_0_), channel_id=1, source_target_pairs={{0,128},{128,0},{1,129},{129,1},{2,130},{130,2},{3,131},{131,3},{4... | collective-permute-start | bytes 3538952 | tf_op jit(solution)/shard_map/ppermute | solution.py:17
  24.0 2.1 %collective-permute-start.1 = (bf16[2,384,768]{2,1,0:T(8,128)(2,1)S(1)}, bf16[2,384,768]{2,1,0:T(8,128)(2,1)S(1)}, u32[]{:S(2)}, u32[]{:S(2)}) collective-permute-start(bf16[2,384,768]{2,1,0:T(8,128)(2,1)S(1)} %pad_maximum_fusion.refs_0_), channel_id=1, source_target_pairs={{0,16},{16,0},{1,17},{17,1},{2,18},{18,2},{3,19},{19,3},{4,20},{20... | collective-permute-start | bytes 3538952 | tf_op jit(solution)/shard_map/ppermute | solution.py:17
  26.1 18.7 %collective-permute-done.4.refs_4_ = bf16[2,384,768]{2,1,0:T(8,128)(2,1)S(1)} collective-permute-done((bf16[2,384,768]{2,1,0:T(8,128)(2,1)S(1)}, bf16[2,384,768]{2,1,0:T(8,128)(2,1)S(1)}, u32[]{:S(2)}, u32[]{:S(2)}) %collective-permute-start.4) | collective-permute-done | bytes 1179680 | tf_op jit(solution)/shard_map/ppermute | solution.py:17
  44.9 3.6 %collective-permute-start.7 = (bf16[384,768]{1,0:T(8,128)(2,1)S(1)}, bf16[384,768]{1,0:T(8,128)(2,1)S(1)}, u32[]{:S(2)}, u32[]{:S(2)}) collective-permute-start(bf16[384,768]{1,0:T(8,128)(2,1)S(1)} %slice_bitcast_fusion), channel_id=1, source_target_pairs={{0,96},{32,0},{64,32},{96,64},{1,97},{33,1},{65,33},{97,65},{2,98}... | collective-permute-start | bytes 1769480 | tf_op jit(solution)/shard_map/ppermute | solution.py:17
  48.4 0.0 collective-permute-done.2.refs_2_
  48.5 0.1 collective-permute-start.6
  48.6 2.7 %collective-permute-start.5 = (bf16[2,384,768]{2,1,0:T(8,128)(2,1)S(1)}, bf16[2,384,768]{2,1,0:T(8,128)(2,1)S(1)}, u32[]{:S(2)}, u32[]{:S(2)}) collective-permute-start(bf16[2,384,768]{2,1,0:T(8,128)(2,1)S(1)} %collective-permute-done.4.refs_4_), channel_id=1, source_target_pairs={{0,16},{16,0},{1,17},{17,1},{2,18},{18,2},{3,19},{19,3},{4,20},{20... | collective-permute-start | bytes 3538952 | tf_op jit(solution)/shard_map/ppermute | solution.py:17
  51.3 0.0 collective-permute-done.9.refs_8_
  51.3 0.1 collective-permute-start.10
  51.4 7.3 %collective-permute-done.7 = bf16[384,768]{1,0:T(8,128)(2,1)S(1)} collective-permute-done((bf16[384,768]{1,0:T(8,128)(2,1)S(1)}, bf16[384,768]{1,0:T(8,128)(2,1)S(1)}, u32[]{:S(2)}, u32[]{:S(2)}) %collective-permute-start.7) | collective-permute-done | bytes 589856 | tf_op jit(solution)/shard_map/ppermute | solution.py:17
  58.7 3.5 %collective-permute-start.13 = (bf16[2,384,768]{2,1,0:T(8,128)(2,1)S(1)}, bf16[2,384,768]{2,1,0:T(8,128)(2,1)S(1)}, u32[]{:S(2)}, u32[]{:S(2)}) collective-permute-start(bf16[2,384,768]{2,1,0:T(8,128)(2,1)S(1)} %collective-permute-done.9.refs_8_), channel_id=1, source_target_pairs={{0,96},{32,0},{64,32},{96,64},{1,97},{33,1},{65,33},{97,65},{2,98}... | collective-permute-start | bytes 3538952 | tf_op jit(solution)/shard_map/ppermute | solution.py:17
  62.2 0.0 collective-permute-done.6
  62.2 0.0 collective-permute-start.11
  62.2 0.0 copy-done.5
  62.2 0.1 pad_maximum_fusion.1.refs_6_
  62.4 0.0 copy-done.7
  62.4 0.0 copy-start.2
  62.4 0.0 collective-permute-done.1.refs_1_
  62.4 0.0 copy-start.8
  62.4 3.0 %collective-permute-start.15 = (bf16[2,384,768]{2,1,0:T(8,128)(2,1)S(1)}, bf16[2,384,768]{2,1,0:T(8,128)(2,1)S(1)}, u32[]{:S(2)}, u32[]{:S(2)}) collective-permute-start(bf16[2,384,768]{2,1,0:T(8,128)(2,1)S(1)} %pad_maximum_fusion.1.refs_6_), channel_id=1, source_target_pairs={{0,128},{128,0},{1,129},{129,1},{2,130},{130,2},{3,131},{131,3},{4... | collective-permute-start | bytes 3538952 | tf_op jit(solution)/shard_map/ppermute | solution.py:17
  65.4 0.0 collective-permute-done.10.refs_9_
  65.4 0.0 copy-done.6
  65.4 3.8 %collective-permute-start.3 = (bf16[2,384,768]{2,1,0:T(8,128)(2,1)S(1)}, bf16[2,384,768]{2,1,0:T(8,128)(2,1)S(1)}, u32[]{:S(2)}, u32[]{:S(2)}) collective-permute-start(bf16[2,384,768]{2,1,0:T(8,128)(2,1)S(1)} %collective-permute-done.2.refs_2_), channel_id=1, source_target_pairs={{0,16},{16,0},{1,17},{17,1},{2,18},{18,2},{3,19},{19,3},{4,20},{20... | collective-permute-start | bytes 3538952 | tf_op jit(solution)/shard_map/ppermute | solution.py:17
  69.2 0.0 collective-permute-done.5.refs_5_
  69.2 0.1 collective-permute-start.8
  69.3 15.0 %collective-permute-done.13.refs_12_ = bf16[2,384,768]{2,1,0:T(8,128)(2,1)S(1)} collective-permute-done((bf16[2,384,768]{2,1,0:T(8,128)(2,1)S(1)}, bf16[2,384,768]{2,1,0:T(8,128)(2,1)S(1)}, u32[]{:S(2)}, u32[]{:S(2)}) %collective-permute-start.13) | collective-permute-done | bytes 1179680 | tf_op jit(solution)/shard_map/ppermute | solution.py:17
  84.3 4.1 %collective-permute-start.14 = (bf16[2,384,768]{2,1,0:T(8,128)(2,1)S(1)}, bf16[2,384,768]{2,1,0:T(8,128)(2,1)S(1)}, u32[]{:S(2)}, u32[]{:S(2)}) collective-permute-start(bf16[2,384,768]{2,1,0:T(8,128)(2,1)S(1)} %collective-permute-done.13.refs_12_), channel_id=1, source_target_pairs={{0,16},{16,0},{1,17},{17,1},{2,18},{18,2},{3,19},{19,3},{4,20},{20... | collective-permute-start | bytes 3538952 | tf_op jit(solution)/shard_map/ppermute | solution.py:17
  88.4 0.0 collective-permute-done.11.refs_10_
  88.4 3.4 %collective-permute-start.12 = (bf16[2,384,768]{2,1,0:T(8,128)(2,1)S(1)}, bf16[2,384,768]{2,1,0:T(8,128)(2,1)S(1)}, u32[]{:S(2)}, u32[]{:S(2)}) collective-permute-start(bf16[2,384,768]{2,1,0:T(8,128)(2,1)S(1)} %collective-permute-done.11.refs_10_), channel_id=1, source_target_pairs={{0,16},{16,0},{1,17},{17,1},{2,18},{18,2},{3,19},{19,3},{4,20},{20... | collective-permute-start | bytes 3538952 | tf_op jit(solution)/shard_map/ppermute | solution.py:17
  91.8 0.0 collective-permute-done.15.refs_14_
  91.8 0.5 collective-permute-start.16
  92.4 0.0 collective-permute-done.3.refs_3_
  92.4 0.0 collective-permute-done.8.refs_7_
  92.4 0.0 copy-done.8
  92.4 0.0 copy-start.15
  92.4 0.0 collective-permute-done.14.refs_13_
  92.4 0.0 copy-done.9
  92.4 0.0 copy-start.16
  92.4 1.9 %collective-permute-done.12.refs_11_ = bf16[2,384,768]{2,1,0:T(8,128)(2,1)S(1)} collective-permute-done((bf16[2,384,768]{2,1,0:T(8,128)(2,1)S(1)}, bf16[2,384,768]{2,1,0:T(8,128)(2,1)S(1)}, u32[]{:S(2)}, u32[]{:S(2)}) %collective-permute-start.12) | collective-permute-done | bytes 1179680 | tf_op jit(solution)/shard_map/ppermute | solution.py:17
  94.3 0.0 copy-done.10
  94.3 0.0 copy-done.11
  94.3 0.0 copy-done.12
  94.3 0.0 copy-done.13
  94.3 0.0 copy-done.14
  94.3 0.0 copy-done.15
  94.3 1.0 copy-done.17
  95.4 0.8 collective-permute-done.16.refs_15_
  96.1 0.9 all-gather.2.cloned.1.call-done.tokens_ref
  97.0 0.0 copy-done.1
  97.0 13.8 %shard_map.37 = f32[512,768]{1,0:T(8,128)} custom-call(bf16[16,512,384]{2,1,0:T(8,128)(2,1)} %all-gather.2.cloned.1.call-done.tokens_ref, bf16[2,384,768]{2,1,0:T(8,128)(2,1)} %copy-done.1, bf16[2,384,768]{2,1,0:T(8,128)(2,1)} %copy-done.8, bf16[2,384,768]{2,1,0:T(8,128)(2,1)} %copy-done.6, bf16[2,384,768]{2,1,0:T(8,128)(2,1)} %copy-done.14, ...), custom_call_target="tpu_custom_call" | custom-call | flops 9663676416 | bytes 26738688 | tf_op jit(solution)/shard_map/pallas_call | solution.py:133
  (16 shorter events, 0.1 us)
Async XLA Ops:
  6.5 3.2 %copy-start.3 = (bf16[384,768]{1,0:T(8,128)(2,1)S(1)}, bf16[384,768]{1,0:T(8,128)(2,1)}, u32[]{:S(2)}) copy-start(bf16[384,768]{1,0:T(8,128)(2,1)} %param.5) | copy-start | bytes 1769476
  6.5 3.2 %copy-start.4 = (bf16[384,768]{1,0:T(8,128)(2,1)S(1)}, bf16[384,768]{1,0:T(8,128)(2,1)}, u32[]{:S(2)}) copy-start(bf16[384,768]{1,0:T(8,128)(2,1)} %param.4) | copy-start | bytes 1769476
  6.5 90.5 %all-gather.2.cloned.1.call-start = ((), (), s32[]{:S(2)}) async-start(), calls=%async_computation | async-start | bytes 7077888 | tf_op jit(solution)/shard_map/all_gather | solution.py:111
  6.5 10.0 %collective-permute-start = (bf16[512,384]{1,0:T(8,128)(2,1)}, bf16[512,384]{1,0:T(8,128)(2,1)S(1)}, u32[]{:S(2)}, u32[]{:S(2)}) collective-permute-start(bf16[512,384]{1,0:T(8,128)(2,1)} %param.3), channel_id=1, source_target_pairs={{0,8},{8,0},{1,9},{9,1},{2,10},{10,2},{3,11},{11,3},{4,12},{12,4},... | collective-permute-start | bytes 1179656 | tf_op jit(solution)/shard_map/ppermute | solution.py:17
  9.9 87.1 %copy-start.1 = (bf16[2,384,768]{2,1,0:T(8,128)(2,1)}, bf16[2,384,768]{2,1,0:T(8,128)(2,1)S(1)}, u32[]{:S(2)}) copy-start(bf16[2,384,768]{2,1,0:T(8,128)(2,1)S(1)} %pad_maximum_fusion.refs_0_) | copy-start | bytes 3538948
  16.6 0.9 copy-start
  17.6 27.3 %collective-permute-start.4 = (bf16[2,384,768]{2,1,0:T(8,128)(2,1)S(1)}, bf16[2,384,768]{2,1,0:T(8,128)(2,1)S(1)}, u32[]{:S(2)}, u32[]{:S(2)}) collective-permute-start(bf16[2,384,768]{2,1,0:T(8,128)(2,1)S(1)} %pad_maximum_fusion.refs_0_), channel_id=1, source_target_pairs={{0,96},{32,0},{64,32},{96,64},{1,97},{33,1},{65,33},{97,65},{2,98}... | collective-permute-start | bytes 3538952 | tf_op jit(solution)/shard_map/ppermute | solution.py:17
  21.1 27.4 %collective-permute-start.2 = (bf16[2,384,768]{2,1,0:T(8,128)(2,1)S(1)}, bf16[2,384,768]{2,1,0:T(8,128)(2,1)S(1)}, u32[]{:S(2)}, u32[]{:S(2)}) collective-permute-start(bf16[2,384,768]{2,1,0:T(8,128)(2,1)S(1)} %pad_maximum_fusion.refs_0_), channel_id=1, source_target_pairs={{0,32},{32,64},{64,96},{96,0},{1,33},{33,65},{65,97},{97,1},{2,34}... | collective-permute-start | bytes 3538952 | tf_op jit(solution)/shard_map/ppermute | solution.py:17
  21.1 30.2 %collective-permute-start.9 = (bf16[2,384,768]{2,1,0:T(8,128)(2,1)S(1)}, bf16[2,384,768]{2,1,0:T(8,128)(2,1)S(1)}, u32[]{:S(2)}, u32[]{:S(2)}) collective-permute-start(bf16[2,384,768]{2,1,0:T(8,128)(2,1)S(1)} %pad_maximum_fusion.refs_0_), channel_id=1, source_target_pairs={{0,128},{128,0},{1,129},{129,1},{2,130},{130,2},{3,131},{131,3},{4... | collective-permute-start | bytes 3538952 | tf_op jit(solution)/shard_map/ppermute | solution.py:17
  24.0 38.4 %collective-permute-start.1 = (bf16[2,384,768]{2,1,0:T(8,128)(2,1)S(1)}, bf16[2,384,768]{2,1,0:T(8,128)(2,1)S(1)}, u32[]{:S(2)}, u32[]{:S(2)}) collective-permute-start(bf16[2,384,768]{2,1,0:T(8,128)(2,1)S(1)} %pad_maximum_fusion.refs_0_), channel_id=1, source_target_pairs={{0,16},{16,0},{1,17},{17,1},{2,18},{18,2},{3,19},{19,3},{4,20},{20... | collective-permute-start | bytes 3538952 | tf_op jit(solution)/shard_map/ppermute | solution.py:17
  44.8 17.4 %copy-start.5 = (bf16[2,384,768]{2,1,0:T(8,128)(2,1)}, bf16[2,384,768]{2,1,0:T(8,128)(2,1)S(1)}, u32[]{:S(2)}) copy-start(bf16[2,384,768]{2,1,0:T(8,128)(2,1)S(1)} %collective-permute-done.4.refs_4_) | copy-start | bytes 3538948
  44.9 13.9 %collective-permute-start.7 = (bf16[384,768]{1,0:T(8,128)(2,1)S(1)}, bf16[384,768]{1,0:T(8,128)(2,1)S(1)}, u32[]{:S(2)}, u32[]{:S(2)}) collective-permute-start(bf16[384,768]{1,0:T(8,128)(2,1)S(1)} %slice_bitcast_fusion), channel_id=1, source_target_pairs={{0,96},{32,0},{64,32},{96,64},{1,97},{33,1},{65,33},{97,65},{2,98}... | collective-permute-start | bytes 1769480 | tf_op jit(solution)/shard_map/ppermute | solution.py:17
  48.5 16.9 %copy-start.6 = (bf16[2,384,768]{2,1,0:T(8,128)(2,1)}, bf16[2,384,768]{2,1,0:T(8,128)(2,1)S(1)}, u32[]{:S(2)}) copy-start(bf16[2,384,768]{2,1,0:T(8,128)(2,1)S(1)} %collective-permute-done.2.refs_2_) | copy-start | bytes 3538948
  48.5 13.7 %collective-permute-start.6 = (bf16[384,768]{1,0:T(8,128)(2,1)S(1)}, bf16[384,768]{1,0:T(8,128)(2,1)S(1)}, u32[]{:S(2)}, u32[]{:S(2)}) collective-permute-start(bf16[384,768]{1,0:T(8,128)(2,1)S(1)} %slice_bitcast_fusion.1), channel_id=1, source_target_pairs={{0,32},{32,64},{64,96},{96,0},{1,33},{33,65},{65,97},{97,1},{2,34}... | collective-permute-start | bytes 1769480 | tf_op jit(solution)/shard_map/ppermute | solution.py:17
  48.6 20.6 %collective-permute-start.5 = (bf16[2,384,768]{2,1,0:T(8,128)(2,1)S(1)}, bf16[2,384,768]{2,1,0:T(8,128)(2,1)S(1)}, u32[]{:S(2)}, u32[]{:S(2)}) collective-permute-start(bf16[2,384,768]{2,1,0:T(8,128)(2,1)S(1)} %collective-permute-done.4.refs_4_), channel_id=1, source_target_pairs={{0,16},{16,0},{1,17},{17,1},{2,18},{18,2},{3,19},{19,3},{4,20},{20... | collective-permute-start | bytes 3538952 | tf_op jit(solution)/shard_map/ppermute | solution.py:17
  51.3 11.0 %copy-start.7 = (bf16[2,384,768]{2,1,0:T(8,128)(2,1)}, bf16[2,384,768]{2,1,0:T(8,128)(2,1)S(1)}, u32[]{:S(2)}) copy-start(bf16[2,384,768]{2,1,0:T(8,128)(2,1)S(1)} %collective-permute-done.9.refs_8_) | copy-start | bytes 3538948
  51.3 14.1 %collective-permute-start.10 = (bf16[2,384,768]{2,1,0:T(8,128)(2,1)S(1)}, bf16[2,384,768]{2,1,0:T(8,128)(2,1)S(1)}, u32[]{:S(2)}, u32[]{:S(2)}) collective-permute-start(bf16[2,384,768]{2,1,0:T(8,128)(2,1)S(1)} %collective-permute-done.9.refs_8_), channel_id=1, source_target_pairs={{0,16},{16,0},{1,17},{17,1},{2,18},{18,2},{3,19},{19,3},{4,20},{20... | collective-permute-start | bytes 3538952 | tf_op jit(solution)/shard_map/ppermute | solution.py:17
  58.7 25.6 %collective-permute-start.13 = (bf16[2,384,768]{2,1,0:T(8,128)(2,1)S(1)}, bf16[2,384,768]{2,1,0:T(8,128)(2,1)S(1)}, u32[]{:S(2)}, u32[]{:S(2)}) collective-permute-start(bf16[2,384,768]{2,1,0:T(8,128)(2,1)S(1)} %collective-permute-done.9.refs_8_), channel_id=1, source_target_pairs={{0,96},{32,0},{64,32},{96,64},{1,97},{33,1},{65,33},{97,65},{2,98}... | collective-permute-start | bytes 3538952 | tf_op jit(solution)/shard_map/ppermute | solution.py:17
  62.2 26.2 %collective-permute-start.11 = (bf16[2,384,768]{2,1,0:T(8,128)(2,1)S(1)}, bf16[2,384,768]{2,1,0:T(8,128)(2,1)S(1)}, u32[]{:S(2)}, u32[]{:S(2)}) collective-permute-start(bf16[2,384,768]{2,1,0:T(8,128)(2,1)S(1)} %collective-permute-done.9.refs_8_), channel_id=1, source_target_pairs={{0,32},{32,64},{64,96},{96,0},{1,33},{33,65},{65,97},{97,1},{2,34}... | collective-permute-start | bytes 3538952 | tf_op jit(solution)/shard_map/ppermute | solution.py:17
  62.4 34.7 %copy-start.2 = (bf16[2,384,768]{2,1,0:T(8,128)(2,1)}, bf16[2,384,768]{2,1,0:T(8,128)(2,1)S(1)}, u32[]{:S(2)}) copy-start(bf16[2,384,768]{2,1,0:T(8,128)(2,1)S(1)} %pad_maximum_fusion.1.refs_6_) | copy-start | bytes 3538948
  62.4 30.0 %copy-start.8 = (bf16[2,384,768]{2,1,0:T(8,128)(2,1)}, bf16[2,384,768]{2,1,0:T(8,128)(2,1)S(1)}, u32[]{:S(2)}) copy-start(bf16[2,384,768]{2,1,0:T(8,128)(2,1)S(1)} %collective-permute-done.1.refs_1_) | copy-start | bytes 3538948
  62.4 29.4 %collective-permute-start.15 = (bf16[2,384,768]{2,1,0:T(8,128)(2,1)S(1)}, bf16[2,384,768]{2,1,0:T(8,128)(2,1)S(1)}, u32[]{:S(2)}, u32[]{:S(2)}) collective-permute-start(bf16[2,384,768]{2,1,0:T(8,128)(2,1)S(1)} %pad_maximum_fusion.1.refs_6_), channel_id=1, source_target_pairs={{0,128},{128,0},{1,129},{129,1},{2,130},{130,2},{3,131},{131,3},{4... | collective-permute-start | bytes 3538952 | tf_op jit(solution)/shard_map/ppermute | solution.py:17
  65.4 28.9 %copy-start.10 = (bf16[2,384,768]{2,1,0:T(8,128)(2,1)}, bf16[2,384,768]{2,1,0:T(8,128)(2,1)S(1)}, u32[]{:S(2)}) copy-start(bf16[2,384,768]{2,1,0:T(8,128)(2,1)S(1)} %collective-permute-done.10.refs_9_) | copy-start | bytes 3538948
  65.4 27.0 %collective-permute-start.3 = (bf16[2,384,768]{2,1,0:T(8,128)(2,1)S(1)}, bf16[2,384,768]{2,1,0:T(8,128)(2,1)S(1)}, u32[]{:S(2)}, u32[]{:S(2)}) collective-permute-start(bf16[2,384,768]{2,1,0:T(8,128)(2,1)S(1)} %collective-permute-done.2.refs_2_), channel_id=1, source_target_pairs={{0,16},{16,0},{1,17},{17,1},{2,18},{18,2},{3,19},{19,3},{4,20},{20... | collective-permute-start | bytes 3538952 | tf_op jit(solution)/shard_map/ppermute | solution.py:17
  69.2 23.2 %copy-start.9 = (bf16[2,384,768]{2,1,0:T(8,128)(2,1)}, bf16[2,384,768]{2,1,0:T(8,128)(2,1)S(1)}, u32[]{:S(2)}) copy-start(bf16[2,384,768]{2,1,0:T(8,128)(2,1)S(1)} %collective-permute-done.5.refs_5_) | copy-start | bytes 3538948
  69.2 23.1 %collective-permute-start.8 = (bf16[2,384,768]{2,1,0:T(8,128)(2,1)S(1)}, bf16[2,384,768]{2,1,0:T(8,128)(2,1)S(1)}, u32[]{:S(2)}, u32[]{:S(2)}) collective-permute-start(bf16[2,384,768]{2,1,0:T(8,128)(2,1)S(1)} %pad_maximum_fusion.1.refs_6_), channel_id=1, source_target_pairs={{0,16},{16,0},{1,17},{17,1},{2,18},{18,2},{3,19},{19,3},{4,20},{20... | collective-permute-start | bytes 3538952 | tf_op jit(solution)/shard_map/ppermute | solution.py:17
  84.3 10.0 %copy-start.11 = (bf16[2,384,768]{2,1,0:T(8,128)(2,1)}, bf16[2,384,768]{2,1,0:T(8,128)(2,1)S(1)}, u32[]{:S(2)}) copy-start(bf16[2,384,768]{2,1,0:T(8,128)(2,1)S(1)} %collective-permute-done.13.refs_12_) | copy-start | bytes 3538948
  84.3 8.1 %collective-permute-start.14 = (bf16[2,384,768]{2,1,0:T(8,128)(2,1)S(1)}, bf16[2,384,768]{2,1,0:T(8,128)(2,1)S(1)}, u32[]{:S(2)}, u32[]{:S(2)}) collective-permute-start(bf16[2,384,768]{2,1,0:T(8,128)(2,1)S(1)} %collective-permute-done.13.refs_12_), channel_id=1, source_target_pairs={{0,16},{16,0},{1,17},{17,1},{2,18},{18,2},{3,19},{19,3},{4,20},{20... | collective-permute-start | bytes 3538952 | tf_op jit(solution)/shard_map/ppermute | solution.py:17
  88.4 5.9 %copy-start.12 = (bf16[2,384,768]{2,1,0:T(8,128)(2,1)}, bf16[2,384,768]{2,1,0:T(8,128)(2,1)S(1)}, u32[]{:S(2)}) copy-start(bf16[2,384,768]{2,1,0:T(8,128)(2,1)S(1)} %collective-permute-done.11.refs_10_) | copy-start | bytes 3538948
  88.4 5.9 %collective-permute-start.12 = (bf16[2,384,768]{2,1,0:T(8,128)(2,1)S(1)}, bf16[2,384,768]{2,1,0:T(8,128)(2,1)S(1)}, u32[]{:S(2)}, u32[]{:S(2)}) collective-permute-start(bf16[2,384,768]{2,1,0:T(8,128)(2,1)S(1)} %collective-permute-done.11.refs_10_), channel_id=1, source_target_pairs={{0,16},{16,0},{1,17},{17,1},{2,18},{18,2},{3,19},{19,3},{4,20},{20... | collective-permute-start | bytes 3538952 | tf_op jit(solution)/shard_map/ppermute | solution.py:17
  91.8 2.5 %copy-start.13 = (bf16[2,384,768]{2,1,0:T(8,128)(2,1)}, bf16[2,384,768]{2,1,0:T(8,128)(2,1)S(1)}, u32[]{:S(2)}) copy-start(bf16[2,384,768]{2,1,0:T(8,128)(2,1)S(1)} %collective-permute-done.15.refs_14_) | copy-start | bytes 3538948
  91.8 4.3 %collective-permute-start.16 = (bf16[2,384,768]{2,1,0:T(8,128)(2,1)S(1)}, bf16[2,384,768]{2,1,0:T(8,128)(2,1)}, u32[]{:S(2)}, u32[]{:S(2)}) collective-permute-start(bf16[2,384,768]{2,1,0:T(8,128)(2,1)S(1)} %collective-permute-done.15.refs_14_), channel_id=1, source_target_pairs={{0,16},{16,0},{1,17},{17,1},{2,18},{18,2},{3,19},{19,3},{4,20},{20... | collective-permute-start | bytes 3538952 | tf_op jit(solution)/shard_map/ppermute | solution.py:17
  92.4 1.9 %copy-start.14 = (bf16[2,384,768]{2,1,0:T(8,128)(2,1)}, bf16[2,384,768]{2,1,0:T(8,128)(2,1)S(1)}, u32[]{:S(2)}) copy-start(bf16[2,384,768]{2,1,0:T(8,128)(2,1)S(1)} %collective-permute-done.3.refs_3_) | copy-start | bytes 3538948
  92.4 1.9 %copy-start.15 = (bf16[2,384,768]{2,1,0:T(8,128)(2,1)}, bf16[2,384,768]{2,1,0:T(8,128)(2,1)S(1)}, u32[]{:S(2)}) copy-start(bf16[2,384,768]{2,1,0:T(8,128)(2,1)S(1)} %collective-permute-done.8.refs_7_) | copy-start | bytes 3538948
  92.4 1.9 %copy-start.16 = (bf16[2,384,768]{2,1,0:T(8,128)(2,1)}, bf16[2,384,768]{2,1,0:T(8,128)(2,1)S(1)}, u32[]{:S(2)}) copy-start(bf16[2,384,768]{2,1,0:T(8,128)(2,1)S(1)} %collective-permute-done.14.refs_13_) | copy-start | bytes 3538948
  94.3 1.0 copy-start.17
Sparse Core Ops, SparseCore 0:
  17.7 79.2 all-gather.1
